TPU v7x, 32 devices: a whole 2x2x4 slice. The times are simulated.
32 devices in a mesh: pipe: 2 (over core), row: 4 (over y, x), col: 4 (over z).
Axes of the slice: x: 2, y: 2, z: 4, core: 2. Of those that a mesh axis runs over, the one named last changes fastest.
Arguments:
- inputs: bfloat16 [2, 1024, 1536], P(None, 'row'), may hold values from -6 to 6
- cotangent: bfloat16 [2, 1024, 1536], P(None, 'row'), may hold values from -6 to 6
- segment_ids: int32 [2, 1024], P(None, 'row'), may hold values from 0 to 3, never falling along the last dimension, each value on 1 to 512 neighbouring positions
- batch_order: int32 [2], replicated, may hold values from 0 to 1, each once
- norm_gain: float32 [2, 1536], P('pipe'), may hold values from 0.5 to 1.5
- gate_proj: bfloat16 [2, 1536, 3072], P('pipe', 'row', 'col'), may hold values from -0.15625 to 0.15625
- value_proj: bfloat16 [2, 1536, 3072], P('pipe', 'row', 'col'), may hold values from -0.15625 to 0.15625
- step_proj: bfloat16 [2, 1536, 48], P('pipe', 'row', 'col'), may hold values from -0.15625 to 0.15625
- state_proj: bfloat16 [2, 1536, 256], P('pipe', 'row'), may hold values from -0.15625 to 0.15625
- conv_value: float32 [2, 4, 3072], P('pipe', None, 'col'), may hold values from -3 to 3
- conv_value_bias: float32 [2, 3072], P('pipe', 'col'), may hold values from -3 to 3
- conv_state: float32 [2, 4, 256], P('pipe'), may hold values from -3 to 3
- conv_state_bias: float32 [2, 256], P('pipe'), may hold values from -3 to 3
- step_bias: float32 [2, 48], P('pipe', 'col'), may hold values from -6 to -2
- decay_log: float32 [2, 48], P('pipe', 'col'), may hold values from 0 to 2.7
- skip_gain: float32 [2, 48], P('pipe', 'col'), may hold values from 0.5 to 1.5
- gate_gain: float32 [2, 3072], P('pipe', 'col'), may hold values from 0.5 to 1.5
- out_proj: bfloat16 [2, 3072, 1536], P('pipe', 'col', 'row'), may hold values from -0.109375 to 0.109375
Outputs:
- layer_outputs: bfloat16 [2, 2, 1024, 1536], P('pipe', None, 'row')
- input_grads: float32 [2, 2, 1024, 1536], P('pipe', None, 'row')
- grad_norm_gain: float32 [2, 1536], P('pipe')
- grad_gate_proj: float32 [2, 1536, 3072], P('pipe', 'row', 'col')
- grad_value_proj: float32 [2, 1536, 3072], P('pipe', 'row', 'col')
- grad_step_proj: float32 [2, 1536, 48], P('pipe', 'row', 'col')
- grad_state_proj: float32 [2, 1536, 256], P('pipe', 'row')
- grad_conv_value: float32 [2, 4, 3072], P('pipe', None, 'col')
- grad_conv_value_bias: float32 [2, 3072], P('pipe', 'col')
- grad_conv_state: float32 [2, 4, 256], P('pipe')
- grad_conv_state_bias: float32 [2, 256], P('pipe')
- grad_step_bias: float32 [2, 48], P('pipe', 'col')
- grad_decay_log: float32 [2, 48], P('pipe', 'col')
- grad_skip_gain: float32 [2, 48], P('pipe', 'col')
- grad_gate_gain: float32 [2, 3072], P('pipe', 'col')
- grad_out_proj: float32 [2, 3072, 1536], P('pipe', 'col', 'row')
Inputs may be any that keep to these rules, and one draw needn't show every extreme that they name: `segment_ids`: document numbers never fall along a sequence; every sequence holds 4 documents, numbered from 0. `batch_order`: each micro-batch is named once.
All inputs are finite; a program needn't handle non-finite values.
Results may differ from a plain program's by a relative error of at most 0.011.
Values may be sent and summed in bfloat16 or wider, within the bound.
No kernel may reach another device: no remote copies, remote signals or barrier semaphores. Data moves between devices by JAX's collectives and lax.ppermute only.
A program may use at most 192 MiB of HBM per device.

v0:
```python
import jax
import jax.numpy as jnp
from jax import lax
from jax.sharding import PartitionSpec as P

EPSILON = 1e-05
PRECISE = lax.Precision.HIGHEST


def passed_along(block, axis, distance):
    devices = range(lax.axis_size(axis))
    route = [(i - distance, i) for i in devices if i - distance in devices]
    return lax.ppermute(block, axis, route)


def entering(part, axis, combine, identity, reverse):
    count = lax.axis_size(axis)
    place = lax.axis_index(axis)
    ahead = count - 1 - place if reverse else place
    gathered = jax.tree.map(lambda a: lax.all_gather(a, axis), part)
    state = jax.tree.map(lambda a, e: jnp.zeros_like(a) + jnp.asarray(e, a.dtype), part, identity)

    def one(hop, state):
        source = count - 1 - hop if reverse else hop
        return combine(
            state, jax.tree.map(lambda a: lax.dynamic_index_in_dim(a, source, 0, False), gathered)
        )

    return lax.fori_loop(0, ahead, one, state)


def pre_norm(values, gain_row):
    scale_row = lax.rsqrt(jnp.mean(values * values, axis=-1, keepdims=True) + EPSILON)
    return values * scale_row * gain_row[None, :]


def causal_conv(values, halo_vals, seg_now, seg_halo, weight, bias_row):
    taps = weight.shape[0]
    length = values.shape[0]
    extended = jnp.concatenate([halo_vals, values], axis=0)
    seg_ext = jnp.concatenate([seg_halo, seg_now], axis=0)
    summed = jnp.zeros_like(values) + bias_row[None, :]
    for offset in range(taps):
        shifted = extended[offset : offset + length]
        same_seg = (seg_ext[offset : offset + length] == seg_now).astype(jnp.float32)
        summed = summed + weight[offset][None, :] * shifted * same_seg[:, None]
    return jax.nn.silu(summed)


def mixer_inputs(
    value_pre,
    state_pre,
    halo_value,
    halo_state,
    conv_vw,
    conv_vb,
    conv_sw,
    conv_sb,
    step_raw,
    step_bias,
    decay_log,
    seg_now,
    seg_halo,
):
    value_conv = causal_conv(value_pre, halo_value, seg_now, seg_halo, conv_vw, conv_vb)
    state_conv = causal_conv(state_pre, halo_state, seg_now, seg_halo, conv_sw, conv_sb)
    half_width = state_conv.shape[1] // 2
    step_size = jax.nn.softplus(step_raw + step_bias[None, :])
    decay_rates = -step_size * jnp.exp(decay_log)[None, :]
    return (
        value_conv,
        state_conv[:, :half_width],
        state_conv[:, half_width:],
        step_size,
        decay_rates,
    )


def decay_sums(decay_rates):
    length = decay_rates.shape[0]
    positions = jnp.arange(length)
    lower = (positions[:, None] >= positions[None, :]).astype(jnp.float32)
    return jnp.dot(lower, decay_rates, precision=PRECISE)


def block_output(
    value_conv,
    b_mat,
    c_mat,
    step_size,
    decay_rates,
    skip_gain,
    gate_act,
    carried,
    seg_now,
    seg_prev,
):
    length, head_count = step_size.shape
    value_heads = value_conv.reshape(length, head_count, -1)
    decay_cum = decay_sums(decay_rates)
    positions = jnp.arange(length)
    same_doc = (positions[:, None] >= positions[None, :]) & (seg_now[:, None] == seg_now[None, :])
    decay_gap = jnp.where(same_doc[:, :, None], decay_cum[:, None, :] - decay_cum[None, :, :], 0.0)
    mixing = jnp.where(same_doc[:, :, None], jnp.exp(decay_gap), 0.0)
    scores = jnp.dot(c_mat, b_mat.T, precision=PRECISE)
    weights = mixing * scores[:, :, None] * step_size[None, :, :]
    result = jnp.einsum("tsh,shp->thp", weights, value_heads, precision=PRECISE)
    carry_in = (seg_now == seg_prev).astype(jnp.float32)[:, None] * jnp.exp(decay_cum)
    result = result + carry_in[:, :, None] * jnp.einsum(
        "tn,hpn->thp", c_mat, carried, precision=PRECISE
    )
    result = result + skip_gain[None, :, None] * value_heads
    gated_out = result.reshape(length, -1) * jax.nn.silu(gate_act)
    return (gated_out, jnp.sum(gated_out * gated_out, axis=1))


def block_state(value_conv, b_mat, step_size, decay_rates, seg_now, seg_prev):
    length, head_count = step_size.shape
    value_heads = value_conv.reshape(length, head_count, -1)
    decay_cum = decay_sums(decay_rates)
    last_cum = decay_cum[length - 1]
    inside = (seg_now == seg_now[length - 1]).astype(jnp.float32)
    lead_weight = inside[:, None] * jnp.exp(last_cum[None, :] - decay_cum) * step_size
    state_local = jnp.einsum("sh,shp,sn->hpn", lead_weight, value_heads, b_mat, precision=PRECISE)
    through = jnp.exp(last_cum) * (seg_now[length - 1] == seg_prev).astype(jnp.float32)
    return (through, state_local)


def join_states(first_part, second_part):
    return (
        first_part[0] * second_part[0],
        second_part[0][:, None, None] * first_part[1] + second_part[1],
    )


def gate_norm(gated_out, sumsq_total, gain_row, norm_width):
    return gated_out * lax.rsqrt(sumsq_total[:, None] / norm_width + EPSILON) * gain_row[None, :]


def gather_weights(gate_proj, value_proj, step_proj, state_proj, out_proj):
    return (
        lax.all_gather(gate_proj[0], "row", axis=0, tiled=True),
        lax.all_gather(value_proj[0], "row", axis=0, tiled=True),
        lax.all_gather(step_proj[0], "row", axis=0, tiled=True),
        lax.all_gather(state_proj[0], "row", axis=0, tiled=True),
        lax.all_gather(out_proj[0], "row", axis=1, tiled=True),
    )


def layer_forward(layer_in, seg_now, gathered, small_params):
    gate_w, value_w, step_w, state_w, out_w = gathered
    gain_in, conv_vw, conv_vb, conv_sw, conv_sb, step_bias, decay_log, skip_gain, gate_gain = (
        small_params
    )
    norm_width = conv_vw.shape[1] * lax.axis_size("col")
    layer_f32 = layer_in.astype(jnp.float32)
    normed, norm_pull = jax.vjp(pre_norm, layer_f32, gain_in)
    normed_b = normed.astype(jnp.bfloat16)
    gate_act = jnp.dot(normed_b, gate_w, preferred_element_type=jnp.float32)
    value_pre = jnp.dot(normed_b, value_w, preferred_element_type=jnp.float32)
    state_pre = jnp.dot(normed_b, state_w, preferred_element_type=jnp.float32)
    step_raw = jnp.dot(normed_b, step_w, preferred_element_type=jnp.float32)
    rim_rows = conv_vw.shape[0] - 1
    halo_value, halo_state, seg_halo = passed_along(
        (value_pre[-rim_rows:], state_pre[-rim_rows:], seg_now[-rim_rows:]), "row", 1
    )

    def inputs_piece(*operands):
        return mixer_inputs(*operands, seg_now, seg_halo)

    mixed, pre_pull = jax.vjp(
        inputs_piece,
        value_pre,
        state_pre,
        halo_value,
        halo_state,
        conv_vw,
        conv_vb,
        conv_sw,
        conv_sb,
        step_raw,
        step_bias,
        decay_log,
    )
    value_conv, b_mat, c_mat, step_size, decay_rates = mixed
    seg_prev = seg_halo[rim_rows - 1]

    def state_piece(*operands):
        return block_state(*operands, seg_now, seg_prev)

    (through, state_local), state_pull = jax.vjp(
        state_piece, value_conv, b_mat, step_size, decay_rates
    )
    identity = (jnp.ones_like(through), jnp.zeros_like(state_local))
    carried = entering((through, state_local), "row", join_states, identity, False)[1]

    def output_piece(*operands):
        return block_output(*operands, seg_now, seg_prev)

    (gated_out, squares), out_pull = jax.vjp(
        output_piece, value_conv, b_mat, c_mat, step_size, decay_rates, skip_gain, gate_act, carried
    )
    sumsq_total = lax.psum(squares, "col")

    def norm_piece(gated_in, total_in, gain_row):
        return gate_norm(gated_in, total_in, gain_row, norm_width)

    branch, gate_pull = jax.vjp(norm_piece, gated_out, sumsq_total, gate_gain)
    return (
        layer_f32,
        normed_b,
        norm_pull,
        pre_pull,
        state_pull,
        out_pull,
        gate_pull,
        branch.astype(jnp.bfloat16),
        through,
        carried,
        identity,
    )


def layer_backward(layer_in, seg_now, gathered, small_params, grad_h):
    saved = layer_forward(layer_in, seg_now, gathered, small_params)
    (
        layer_f32,
        normed_b,
        norm_pull,
        pre_pull,
        state_pull,
        out_pull,
        gate_pull,
        branch_b,
        through,
        carried,
        identity,
    ) = saved
    gate_w, value_w, step_w, state_w, out_w = gathered
    grad_out = grad_h.astype(jnp.bfloat16)
    grad_out_w = jnp.einsum("ti,td->id", branch_b, grad_out, preferred_element_type=jnp.float32)
    grad_branch = jnp.einsum("td,id->ti", grad_out, out_w, preferred_element_type=jnp.float32)
    grad_gated, grad_total_part, grad_gate_gain = gate_pull(grad_branch)
    grad_total = lax.psum(grad_total_part, "col")
    out_value, out_bmat, out_cmat, out_step, out_rate, grad_skip, grad_gate_act, grad_carried = (
        out_pull((grad_gated, grad_total))
    )
    adjoint = entering((through, grad_carried), "row", join_states, identity, True)[1]
    grad_through = jnp.sum(adjoint * carried, axis=(1, 2))
    st_value, st_bmat, st_step, st_rate = state_pull((grad_through, adjoint))
    pre_grads = pre_pull(
        (out_value + st_value, out_bmat + st_bmat, out_cmat, out_step + st_step, out_rate + st_rate)
    )
    (
        grad_value_pre,
        grad_state_pre,
        grad_halo_value,
        grad_halo_state,
        grad_conv_vw,
        grad_conv_vb,
        grad_conv_sw,
        grad_conv_sb,
        grad_step_raw,
        grad_step_bias,
        grad_decay_log,
    ) = pre_grads
    from_value, from_state = passed_along((grad_halo_value, grad_halo_state), "row", -1)
    length = grad_value_pre.shape[0]
    rim_rows = from_value.shape[0]
    grad_value_pre = grad_value_pre + jnp.pad(from_value, ((length - rim_rows, 0), (0, 0)))
    grad_state_pre = grad_state_pre + jnp.pad(from_state, ((length - rim_rows, 0), (0, 0)))
    gate_low = grad_gate_act.astype(jnp.bfloat16)
    value_low = grad_value_pre.astype(jnp.bfloat16)
    step_low = grad_step_raw.astype(jnp.bfloat16)
    partial_in = jnp.einsum("ti,di->td", gate_low, gate_w, preferred_element_type=jnp.float32)
    partial_in = partial_in + jnp.einsum(
        "ti,di->td", value_low, value_w, preferred_element_type=jnp.float32
    )
    partial_in = partial_in + jnp.einsum(
        "th,dh->td", step_low, step_w, preferred_element_type=jnp.float32
    )
    sum_in, sum_state, sum_conv_sw, sum_conv_sb = lax.psum(
        (partial_in, grad_state_pre, grad_conv_sw, grad_conv_sb), "col"
    )
    state_low = sum_state.astype(jnp.bfloat16)
    grad_normed = sum_in + jnp.einsum(
        "tc,dc->td", state_low, state_w, preferred_element_type=jnp.float32
    )
    grad_from_norm, grad_gain_in = norm_pull(grad_normed)
    grad_input = grad_h + grad_from_norm
    big_terms = (
        jnp.einsum("td,ti->di", normed_b, gate_low, preferred_element_type=jnp.float32),
        jnp.einsum("td,ti->di", normed_b, value_low, preferred_element_type=jnp.float32),
        jnp.einsum("td,th->dh", normed_b, step_low, preferred_element_type=jnp.float32),
        jnp.einsum("td,tc->dc", normed_b, state_low, preferred_element_type=jnp.float32),
        grad_out_w,
    )
    small_terms = (
        grad_gain_in,
        grad_conv_vw,
        grad_conv_vb,
        sum_conv_sw,
        sum_conv_sb,
        grad_step_bias,
        grad_decay_log,
        grad_skip,
        grad_gate_gain,
    )
    return (big_terms, small_terms, grad_input)


def local(
    inputs,
    cotangent,
    segment_ids,
    batch_order,
    norm_gain,
    gate_proj,
    value_proj,
    step_proj,
    state_proj,
    conv_value,
    conv_value_bias,
    conv_state,
    conv_state_bias,
    step_bias,
    decay_log,
    skip_gain,
    gate_gain,
    out_proj,
):
    section_index = lax.axis_index("pipe")
    section_count = lax.axis_size("pipe")
    micro_count = inputs.shape[0]
    step_count = micro_count + section_count - 1
    small_params = (
        norm_gain[0],
        conv_value[0],
        conv_value_bias[0],
        conv_state[0],
        conv_state_bias[0],
        step_bias[0],
        decay_log[0],
        skip_gain[0],
        gate_gain[0],
    )
    gathered = gather_weights(gate_proj, value_proj, step_proj, state_proj, out_proj)
    seg_all = segment_ids.astype(jnp.float32)
    out_weight = gathered[4]

    def forward_step(received, step_now):
        batch_slot = jnp.clip(step_now - section_index, 0, micro_count - 1)
        source_row = batch_order[batch_slot]
        layer_in = jnp.where(section_index == 0, inputs[source_row], received)
        saved = layer_forward(layer_in, seg_all[source_row], gathered, small_params)
        branch_part = jnp.dot(saved[7], out_weight, preferred_element_type=jnp.float32)
        branch_total = lax.psum(branch_part, "col")
        layer_out = (saved[0] + branch_total).astype(jnp.bfloat16)
        passed = passed_along(layer_out, "pipe", 1)
        return (passed, (layer_in, layer_out))

    zero_rows = jnp.zeros_like(inputs[0])
    last_sent, (inputs_all, outputs_all) = lax.scan(forward_step, zero_rows, jnp.arange(step_count))
    section_inputs = lax.dynamic_slice_in_dim(inputs_all, section_index, micro_count, 0)
    layer_outputs = lax.dynamic_slice_in_dim(outputs_all, section_index, micro_count, 0)
    back_weights = gather_weights(gate_proj, value_proj, step_proj, state_proj, out_proj)
    full_zero = tuple((jnp.zeros(weight.shape, jnp.float32) for weight in back_weights))
    small_zero = tuple((jnp.zeros_like(param) for param in small_params))

    def backward_step(carried_pair, step_now):
        received, big_sums, small_sums = carried_pair
        slot_raw = step_now - (section_count - 1 - section_index)
        batch_slot = jnp.clip(slot_raw, 0, micro_count - 1)
        valid_mask = ((slot_raw >= 0) & (slot_raw < micro_count)).astype(jnp.float32)
        source_row = batch_order[batch_slot]
        grad_h = jnp.where(
            section_index == section_count - 1, cotangent[batch_slot], received
        ).astype(jnp.float32)
        big_terms, small_terms, grad_input = layer_backward(
            section_inputs[batch_slot], seg_all[source_row], back_weights, small_params, grad_h
        )
        big_terms = tuple((addend * valid_mask for addend in big_terms))
        small_sums = tuple(
            (running + addend * valid_mask for running, addend in zip(small_sums, small_terms))
        )
        big_sums = tuple((running + addend for running, addend in zip(big_sums, big_terms)))
        passed = passed_along(grad_input.astype(jnp.bfloat16), "pipe", -1)
        return ((passed, big_sums, small_sums), grad_input)

    (last_back, big_sums, small_sums), grads_all = lax.scan(
        backward_step, (zero_rows, full_zero, small_zero), jnp.arange(step_count)
    )
    section_grads = lax.dynamic_slice_in_dim(
        grads_all, section_count - 1 - section_index, micro_count, 0
    )
    inverse = jnp.argsort(batch_order)
    input_grads = jnp.where(section_index == 0, section_grads[inverse], section_grads)
    big_shares = (
        lax.psum_scatter(big_sums[0], "row", scatter_dimension=0, tiled=True),
        lax.psum_scatter(big_sums[1], "row", scatter_dimension=0, tiled=True),
        lax.psum_scatter(big_sums[2], "row", scatter_dimension=0, tiled=True),
        lax.psum_scatter(big_sums[3], "row", scatter_dimension=0, tiled=True),
        lax.psum_scatter(big_sums[4], "row", scatter_dimension=1, tiled=True),
    )
    small_total = lax.psum(small_sums, "row")
    return (
        layer_outputs[None],
        input_grads[None],
        small_total[0][None],
        big_shares[0][None],
        big_shares[1][None],
        big_shares[2][None],
        big_shares[3][None],
        small_total[1][None],
        small_total[2][None],
        small_total[3][None],
        small_total[4][None],
        small_total[5][None],
        small_total[6][None],
        small_total[7][None],
        small_total[8][None],
        big_shares[4][None],
    )


def solution(mesh):
    in_specs = (
        P(None, "row", None),
        P(None, "row", None),
        P(None, "row"),
        P(),
        P("pipe", None),
        P("pipe", "row", "col"),
        P("pipe", "row", "col"),
        P("pipe", "row", "col"),
        P("pipe", "row", None),
        P("pipe", None, "col"),
        P("pipe", "col"),
        P("pipe", None, None),
        P("pipe", None),
        P("pipe", "col"),
        P("pipe", "col"),
        P("pipe", "col"),
        P("pipe", "col"),
        P("pipe", "col", "row"),
    )
    out_specs = (
        P("pipe", None, "row", None),
        P("pipe", None, "row", None),
        P("pipe", None),
        P("pipe", "row", "col"),
        P("pipe", "row", "col"),
        P("pipe", "row", "col"),
        P("pipe", "row", None),
        P("pipe", None, "col"),
        P("pipe", "col"),
        P("pipe", None, None),
        P("pipe", None),
        P("pipe", "col"),
        P("pipe", "col"),
        P("pipe", "col"),
        P("pipe", "col"),
        P("pipe", "col", "row"),
    )
    return jax.shard_map(local, mesh=mesh, in_specs=in_specs, out_specs=out_specs, check_vma=False)
```

profile of v0, /device:TPU:0, one launch (start us, length us, event | category | flops | bytes accessed | tf_op | source)
XLA Modules:
  0.0 1715.9 jit_solution(2911276389352426753)
XLA Ops:
  35.5 17.8 %all-gather.30.cloned.1.call-done = bf16[1,1536,768]{2,1,0:T(8,128)(2,1)} async-done(((bf16[1,384,768]{2,1,0:T(8,128)(2,1)}), bf16[1,1536,768]{2,1,0:T(8,128)(2,1)}) %all-gather.30.cloned.1.call-update) | async-done | bytes 2359312 | tf_op jit(solution)/shard_map/all_gather | solution.py:143
  53.3 39.3 %all-gather.32.cloned.1.call-done = bf16[1,1536,768]{2,1,0:T(8,128)(2,1)} async-done(((bf16[1,384,768]{2,1,0:T(8,128)(2,1)}), bf16[1,1536,768]{2,1,0:T(8,128)(2,1)}) %all-gather.32.cloned.1.call-update) | async-done | bytes 2359312 | tf_op jit(solution)/shard_map/all_gather | solution.py:142
  92.7 39.2 %all-gather.34.cloned.1.call-done = bf16[1,768,1536]{2,1,0:T(8,128)(2,1)} async-done(((bf16[1,768,384]{2,1,0:T(8,128)(2,1)}), bf16[1,768,1536]{2,1,0:T(8,128)(2,1)}) %all-gather.34.cloned.1.call-update) | async-done | bytes 2359312 | tf_op jit(solution)/shard_map/all_gather | solution.py:146
  132.8 477.3 %while.116 = (s32[]{:T(128)}, bf16[256,1536]{1,0:T(8,128)(2,1)}, bf16[3,256,1536]{2,1,0:T(8,128)(2,1)}, bf16[3,256,1536]{2,1,0:T(8,128)(2,1)}, pred[]{:T(512)}, ...) while((s32[]{:T(128)}, bf16[256,1536]{1,0:T(8,128)(2,1)}, ...), condition=%wide.region_7.8_spmd, body=%wide.region_0.7_spmd.sunk | while | flops 3363548160 | bytes 76281928 | solution.py:363
  177.4 17.2 %all-gather.36.cloned.1.call-done = f32[48,64,128]{2,1,0:T(8,128)} async-done(((f32[12,64,128]{2,1,0:T(8,128)}), f32[48,64,128]{2,1,0:T(8,128)}) %all-gather.36.cloned.1.call-update) | async-done | bytes 1572880 | tf_op jit(solution)/shard_map/while/body/eval_jaxpr/all_gather | solution.py:20
  216.1 69.4 %all-reduce.29.cloned.1.call-done = f32[256,1536]{1,0:T(8,128)} async-done(((f32[256,1536]{1,0:T(8,128)}), f32[256,1536]{1,0:T(8,128)}) %all-reduce.29.cloned.1.call-update) | async-done | bytes 1572880 | tf_op jit(solution)/shard_map/while/body/eval_jaxpr/psum | solution.py:357
  337.6 16.1 all-gather.36.cloned.1.call-done
  375.2 69.4 %all-reduce.29.cloned.1.call-done = f32[256,1536]{1,0:T(8,128)} async-done(((f32[256,1536]{1,0:T(8,128)}), f32[256,1536]{1,0:T(8,128)}) %all-reduce.29.cloned.1.call-update) | async-done | bytes 1572880 | tf_op jit(solution)/shard_map/while/body/eval_jaxpr/psum | solution.py:357
  534.2 69.4 %all-reduce.29.cloned.1.call-done = f32[256,1536]{1,0:T(8,128)} async-done(((f32[256,1536]{1,0:T(8,128)}), f32[256,1536]{1,0:T(8,128)}) %all-reduce.29.cloned.1.call-update) | async-done | bytes 1572880 | tf_op jit(solution)/shard_map/while/body/eval_jaxpr/psum | solution.py:357
  612.7 852.9 %while.119 = (s32[]{:T(128)}, bf16[256,1536]{1,0:T(8,128)(2,1)}, f32[1536,768]{1,0:T(8,128)}, f32[1536,768]{1,0:T(8,128)}, f32[1536,12]{0,1:T(8,128)}, /*index=5...) while((s32[]{:T(128)}, bf16[256,1536]{1,0:T(8,128)(2,1)}, ...), condition=%wide.region_46.47_spmd.clone, body=%wide.region_8.46_spmd.clone.sunk | while | flops 9502610432 | bytes 227824960 | solution.py:390
  681.7 18.0 %all-gather.38.cloned.1.call-done = f32[48,64,128]{2,1,0:T(8,128)} async-done(((f32[12,64,128]{2,1,0:T(8,128)}), f32[48,64,128]{2,1,0:T(8,128)}) %all-gather.38.cloned.1.call-update) | async-done | bytes 1572880 | tf_op jit(solution)/shard_map/while/body/eval_jaxpr/all_gather | solution.py:20
  826.2 35.2 %all-reduce.32 = (bf16[256,256]{1,0:T(8,128)(2,1)S(1)}, f32[4,256]{1,0:T(4,128)S(1)}, f32[256]{0:T(256)S(1)}) all-reduce(f32[256,256]{1,0:T(8,128)} %slice_add_fusion.3, f32[4,256]{1,0:T(4,128)S(1)} %pad_add_fusion.14, f32[256]{0:T(256)S(1)} %copy-done.115), channel_id=1, replica_groups=mesh['pipe'=2,'row'=4,'col'=4] {'col'}, use_global_device_ids=true, to_apply=%region_26.26 | all-reduce | flops 66816 | bytes 403456 | tf_op jit(solution)/shard_map/while/body/eval_jaxpr/psum | solution.py:282
  866.3 38.2 %all-reduce.31.cloned.1.call-done = f32[256,1536]{1,0:T(8,128)} async-done(((f32[256,1536]{1,0:T(8,128)}), f32[256,1536]{1,0:T(8,128)}) %all-reduce.31.cloned.1.call-update) | async-done | bytes 1572880 | tf_op jit(solution)/shard_map/while/body/eval_jaxpr/psum | solution.py:282
  957.9 17.4 %all-gather.38.cloned.1.call-done = f32[48,64,128]{2,1,0:T(8,128)} async-done(((f32[12,64,128]{2,1,0:T(8,128)}), f32[48,64,128]{2,1,0:T(8,128)}) %all-gather.38.cloned.1.call-update) | async-done | bytes 1572880 | tf_op jit(solution)/shard_map/while/body/eval_jaxpr/all_gather | solution.py:20
  1102.6 35.3 %all-reduce.32 = (bf16[256,256]{1,0:T(8,128)(2,1)S(1)}, f32[4,256]{1,0:T(4,128)S(1)}, f32[256]{0:T(256)S(1)}) all-reduce(f32[256,256]{1,0:T(8,128)} %slice_add_fusion.3, f32[4,256]{1,0:T(4,128)S(1)} %pad_add_fusion.14, f32[256]{0:T(256)S(1)} %copy-done.115), channel_id=1, replica_groups=mesh['pipe'=2,'row'=4,'col'=4] {'col'}, use_global_device_ids=true, to_apply=%region_26.26 | all-reduce | flops 66816 | bytes 403456 | tf_op jit(solution)/shard_map/while/body/eval_jaxpr/psum | solution.py:282
  1146.7 34.4 %all-reduce.31.cloned.1.call-done = f32[256,1536]{1,0:T(8,128)} async-done(((f32[256,1536]{1,0:T(8,128)}), f32[256,1536]{1,0:T(8,128)}) %all-reduce.31.cloned.1.call-update) | async-done | bytes 1572880 | tf_op jit(solution)/shard_map/while/body/eval_jaxpr/psum | solution.py:282
  1234.4 17.4 %all-gather.38.cloned.1.call-done = f32[48,64,128]{2,1,0:T(8,128)} async-done(((f32[12,64,128]{2,1,0:T(8,128)}), f32[48,64,128]{2,1,0:T(8,128)}) %all-gather.38.cloned.1.call-update) | async-done | bytes 1572880 | tf_op jit(solution)/shard_map/while/body/eval_jaxpr/all_gather | solution.py:20
  1379.1 35.3 %all-reduce.32 = (bf16[256,256]{1,0:T(8,128)(2,1)S(1)}, f32[4,256]{1,0:T(4,128)S(1)}, f32[256]{0:T(256)S(1)}) all-reduce(f32[256,256]{1,0:T(8,128)} %slice_add_fusion.3, f32[4,256]{1,0:T(4,128)S(1)} %pad_add_fusion.14, f32[256]{0:T(256)S(1)} %copy-done.115), channel_id=1, replica_groups=mesh['pipe'=2,'row'=4,'col'=4] {'col'}, use_global_device_ids=true, to_apply=%region_26.26 | all-reduce | flops 66816 | bytes 403456 | tf_op jit(solution)/shard_map/while/body/eval_jaxpr/psum | solution.py:282
  1423.2 34.4 %all-reduce.31.cloned.1.call-done = f32[256,1536]{1,0:T(8,128)} async-done(((f32[256,1536]{1,0:T(8,128)}), f32[256,1536]{1,0:T(8,128)}) %all-reduce.31.cloned.1.call-update) | async-done | bytes 1572880 | tf_op jit(solution)/shard_map/while/body/eval_jaxpr/psum | solution.py:282
  1477.0 16.9 all-reduce.22
  1502.0 24.1 %reduce-scatter.12.cloned.1.call-done = f32[384,256]{1,0:T(8,128)} async-done(((f32[1536,256]{1,0:T(8,128)}), f32[384,256]{1,0:T(8,128)}) %reduce-scatter.12.cloned.1.call-update) | async-done | bytes 393232 | tf_op jit(solution)/shard_map/reduce_scatter | solution.py:402
  1526.2 61.0 %reduce-scatter.6.cloned.1.call-done = f32[384,768]{1,0:T(8,128)} async-done(((f32[1536,768]{1,0:T(8,128)}), f32[384,768]{1,0:T(8,128)}) %reduce-scatter.6.cloned.1.call-update) | async-done | bytes 1179664 | tf_op jit(solution)/shard_map/reduce_scatter | solution.py:399
  1587.1 60.9 %reduce-scatter.8.cloned.1.call-done = f32[384,768]{1,0:T(8,128)} async-done(((f32[1536,768]{1,0:T(8,128)}), f32[384,768]{1,0:T(8,128)}) %reduce-scatter.8.cloned.1.call-update) | async-done | bytes 1179664 | tf_op jit(solution)/shard_map/reduce_scatter | solution.py:400
  1648.1 60.9 %reduce-scatter.14.cloned.1.call-done = f32[768,384]{1,0:T(8,128)} async-done(((f32[768,1536]{1,0:T(8,128)}), f32[768,384]{1,0:T(8,128)}) %reduce-scatter.14.cloned.1.call-update) | async-done | bytes 1179664 | tf_op jit(solution)/shard_map/reduce_scatter | solution.py:403
  (1437 shorter events, 837.2 us)
Async XLA Ops:
  7.2 46.1 %all-gather.30.cloned.1.call-start = ((), (), s32[]{:S(2)}) async-start(), calls=%async_computation.10 | async-start | bytes 2949120 | tf_op jit(solution)/shard_map/all_gather | solution.py:143
  8.0 84.7 %all-gather.32.cloned.1.call-start = ((), (), s32[]{:S(2)}) async-start(), calls=%async_computation.11 | async-start | bytes 2949120 | tf_op jit(solution)/shard_map/all_gather | solution.py:142
  8.7 123.1 %all-gather.34.cloned.1.call-start = ((), (), s32[]{:S(2)}) async-start(), calls=%async_computation.12 | async-start | bytes 2949120 | tf_op jit(solution)/shard_map/all_gather | solution.py:146
  132.8 61.8 %all-gather.36.cloned.1.call-start = ((), (), s32[]{:S(2)}) async-start(), calls=%async_computation.13 | async-start | bytes 1966080 | tf_op jit(solution)/shard_map/while/body/eval_jaxpr/all_gather | solution.py:20
  164.4 121.1 %all-reduce.29.cloned.1.call-start = ((), (), s32[]{:S(2)}) async-start(), calls=%async_computation.14 | async-start | bytes 3145728 | tf_op jit(solution)/shard_map/while/body/eval_jaxpr/psum | solution.py:357
  292.2 61.5 %all-gather.36.cloned.1.call-start = ((), (), s32[]{:S(2)}) async-start(), calls=%async_computation.13 | async-start | bytes 1966080 | tf_op jit(solution)/shard_map/while/body/eval_jaxpr/all_gather | solution.py:20
  324.6 120.0 %all-reduce.29.cloned.1.call-start = ((), (), s32[]{:S(2)}) async-start(), calls=%async_computation.14 | async-start | bytes 3145728 | tf_op jit(solution)/shard_map/while/body/eval_jaxpr/psum | solution.py:357
  451.2 61.4 %all-gather.36.cloned.1.call-start = ((), (), s32[]{:S(2)}) async-start(), calls=%async_computation.13 | async-start | bytes 1966080 | tf_op jit(solution)/shard_map/while/body/eval_jaxpr/all_gather | solution.py:20
  460.1 21.1 %collective-permute-start.6 = (f32[3,768]{1,0:T(4,128)S(1)}, f32[3,768]{1,0:T(4,128)S(1)}, u32[]{:S(2)}, u32[]{:S(2)}) collective-permute-start(f32[3,768]{1,0:T(4,128)S(1)} %slice.594), channel_id=1, source_target_pairs={{0,4},{4,8},{8,12},{1,5},{5,9},{9,13},{2,6},{6,10},{10,14},{3,7},{... | collective-permute-start | bytes 27656 | tf_op jit(solution)/shard_map/while/body/eval_jaxpr/ppermute | solution.py:13
  483.7 119.8 %all-reduce.29.cloned.1.call-start = ((), (), s32[]{:S(2)}) async-start(), calls=%async_computation.14 | async-start | bytes 3145728 | tf_op jit(solution)/shard_map/while/body/eval_jaxpr/psum | solution.py:357
  636.4 63.3 %all-gather.38.cloned.1.call-start = ((), (), s32[]{:S(2)}) async-start(), calls=%async_computation.15 | async-start | bytes 1966080 | tf_op jit(solution)/shard_map/while/body/eval_jaxpr/all_gather | solution.py:20
  670.7 117.1 %all-gather.40.cloned.1.call-start = ((), (), s32[]{:S(2)}) async-start(), calls=%async_computation.16 | async-start | bytes 1966080 | tf_op jit(solution)/shard_map/while/body/eval_jaxpr/all_gather | solution.py:20
  752.6 151.9 %all-reduce.31.cloned.1.call-start = ((), (), s32[]{:S(2)}) async-start(), calls=%async_computation.17 | async-start | bytes 3145728 | tf_op jit(solution)/shard_map/while/body/eval_jaxpr/psum | solution.py:282
  912.6 62.7 %all-gather.38.cloned.1.call-start = ((), (), s32[]{:S(2)}) async-start(), calls=%async_computation.15 | async-start | bytes 1966080 | tf_op jit(solution)/shard_map/while/body/eval_jaxpr/all_gather | solution.py:20
  946.9 116.5 %all-gather.40.cloned.1.call-start = ((), (), s32[]{:S(2)}) async-start(), calls=%async_computation.16 | async-start | bytes 1966080 | tf_op jit(solution)/shard_map/while/body/eval_jaxpr/all_gather | solution.py:20
  1028.2 152.8 %all-reduce.31.cloned.1.call-start = ((), (), s32[]{:S(2)}) async-start(), calls=%async_computation.17 | async-start | bytes 3145728 | tf_op jit(solution)/shard_map/while/body/eval_jaxpr/psum | solution.py:282
  1189.1 62.7 %all-gather.38.cloned.1.call-start = ((), (), s32[]{:S(2)}) async-start(), calls=%async_computation.15 | async-start | bytes 1966080 | tf_op jit(solution)/shard_map/while/body/eval_jaxpr/all_gather | solution.py:20
  1223.4 116.5 %all-gather.40.cloned.1.call-start = ((), (), s32[]{:S(2)}) async-start(), calls=%async_computation.16 | async-start | bytes 1966080 | tf_op jit(solution)/shard_map/while/body/eval_jaxpr/all_gather | solution.py:20
  1304.8 152.8 %all-reduce.31.cloned.1.call-start = ((), (), s32[]{:S(2)}) async-start(), calls=%async_computation.17 | async-start | bytes 3145728 | tf_op jit(solution)/shard_map/while/body/eval_jaxpr/psum | solution.py:282
  1465.6 35.1 %reduce-scatter.10.cloned.1.call-start = ((), (), s32[]{:S(2)}) async-start(), calls=%async_computation.7 | async-start | bytes 122880 | tf_op jit(solution)/shard_map/reduce_scatter | solution.py:401
  1466.3 59.8 %reduce-scatter.12.cloned.1.call-start = ((), (), s32[]{:S(2)}) async-start(), calls=%async_computation.8 | async-start | bytes 1966080 | tf_op jit(solution)/shard_map/reduce_scatter | solution.py:402
  1466.9 120.2 %reduce-scatter.6.cloned.1.call-start = ((), (), s32[]{:S(2)}) async-start(), calls=%async_computation.5 | async-start | bytes 5898240 | tf_op jit(solution)/shard_map/reduce_scatter | solution.py:399
  1467.7 180.4 %reduce-scatter.8.cloned.1.call-start = ((), (), s32[]{:S(2)}) async-start(), calls=%async_computation.6 | async-start | bytes 5898240 | tf_op jit(solution)/shard_map/reduce_scatter | solution.py:400
  1468.4 240.6 %reduce-scatter.14.cloned.1.call-start = ((), (), s32[]{:S(2)}) async-start(), calls=%async_computation.9 | async-start | bytes 5898240 | tf_op jit(solution)/shard_map/reduce_scatter | solution.py:403
  (454 other events, 3589.6 us)
Sparse Core Ops, SparseCore 0:
  9.9 43.3 all-gather.29
  55.2 37.4 all-gather.31
  94.5 37.3 all-gather.33
  164.5 30.0 all-gather.35
  216.2 69.2 all-reduce.28
  324.7 28.9 all-gather.35
  375.3 69.2 all-reduce.28
  483.8 28.7 all-gather.35
  534.3 69.1 all-reduce.28
  670.8 28.7 all-gather.37
  752.8 34.9 all-gather.39
  824.0 80.4 all-reduce.30
  947.0 28.1 all-gather.37
  1028.4 34.9 all-gather.39
  1100.4 80.5 all-reduce.30
  1223.5 28.2 all-gather.37
  1304.9 34.9 all-gather.39
  1376.9 80.5 all-reduce.30
  1469.2 22.2 reduce-scatter.9
  1495.2 30.9 reduce-scatter.11
  1530.0 57.0 reduce-scatter.5
  1590.9 57.0 reduce-scatter.7
  1651.9 57.0 reduce-scatter.13
where the time goes:
time: 1730 us; the launch traced here: 1720 us
  waiting for transfers between devices  756 us (44%)
  blocking collectives  287 us (17%)
  matrix products  278 us (16%)
  other arithmetic  145 us (8%)
  local copies, waits for them, and re-layouts  104 us (6%)
  starting transfers between devices  77.9 us (5%)
  loops' own time  53.4 us (3%)
    psum x3, waiting for transfers between devices, forward_step(): branch_total = lax.psum(branch_part, 'col')  208 us
    all_gather x9, waiting for transfers between devices, entering(): gathered = jax.tree.map(lambda a: lax.all_gather(a, axis), part)  123 us
    psum x3, waiting for transfers between devices, layer_backward(): lax.psum((partial_in, grad_state_pre, grad_conv_sw, grad_conv_sb), 'col')  107 us
    psum x3, blocking collectives, layer_backward(): lax.psum((partial_in, grad_state_pre, grad_conv_sw, grad_conv_sb), 'col')  106 us
    ppermute x30, starting transfers between devices, passed_along(): return lax.ppermute(block, axis, route)  76.9 us
    psum x6, blocking collectives, layer_forward(): sumsq_total = lax.psum(squares, 'col')  72.1 us
    dot_general x12, matrix products, block_output(): result = jnp.einsum('tsh,shp->thp', weights, value_heads, precision=PRECISE)  65.3 us
    reduce_scatter x1, waiting for transfers between devices, local(): lax.psum_scatter(big_sums[0], 'row', scatter_dimension=0, tiled=True)  61 us
  transfers between devices with their start and end apart: 53, of which 32 were waited for; matrix products, arithmetic and copies ran while one was open for 15% of the time, Pallas kernels for 0%

commit v1 on v0

v1 whole, which is shorter than its diff:
```python
import functools
import math

import jax
import jax.numpy as jnp
from jax import lax
from jax.experimental import pallas as pl
from jax.experimental.pallas import tpu as pltpu
from jax.sharding import PartitionSpec as P

EPSILON = 1e-05
LOG2E = math.log2(math.e)
LANE = 128
F32 = jnp.float32
BF16 = jnp.bfloat16
SMALL_ROWS = 16


def dot_nn(a, b):
    return lax.dot_general(a, b, (((1,), (0,)), ((), ())), preferred_element_type=F32)


def dot_nt(a, b):
    return lax.dot_general(a, b, (((1,), (1,)), ((), ())), preferred_element_type=F32)


def dot_tn(a, b):
    return lax.dot_general(a, b, (((0,), (0,)), ((), ())), preferred_element_type=F32)


def dot_exact(a, b):
    return lax.dot_general(
        a, b, (((1,), (0,)), ((), ())), precision=lax.Precision.HIGHEST, preferred_element_type=F32
    )


def sigmoid(v):
    return 1.0 / (1.0 + jnp.exp(-v))


def split_pair(v):
    high = v.astype(BF16)
    return high, (v - high.astype(F32)).astype(BF16)


def on_chip(kernel, out_shapes, scratch=()):
    whole = pl.BlockSpec(memory_space=pltpu.VMEM)

    def call(*operands):
        return pl.pallas_call(
            kernel,
            out_shape=out_shapes,
            in_specs=[whole] * len(operands),
            out_specs=jax.tree.map(lambda _: whole, out_shapes),
            scratch_shapes=scratch,
            compiler_params=pltpu.CompilerParams(vmem_limit_bytes=60 * 1024 * 1024),
        )(*operands)

    return call


def shaped(shape, dtype=F32):
    return jax.ShapeDtypeStruct(shape, dtype)


def tile_of(q):
    return slice(q * LANE, (q + 1) * LANE)


def spread(columns, q, heads_tile, lane_head):
    first = q * heads_tile
    out = columns[:, first : first + 1]
    for i in range(1, heads_tile):
        out = jnp.where(lane_head == i, columns[:, first + i : first + i + 1], out)
    return out


def lane_heads(rows, heads_tile):
    lanes = lax.broadcasted_iota(jnp.int32, (rows, LANE), 1)
    return lanes // (LANE // heads_tile)


def tri_mask(tokens, seg_col, seg_row, transposed):
    first = lax.broadcasted_iota(jnp.int32, (tokens, tokens), 0)
    second = lax.broadcasted_iota(jnp.int32, (tokens, tokens), 1)
    order = first <= second if transposed else first >= second
    return order & (seg_col == seg_row)


def prep_kernel(
    inner, heads_tile, z_ref, halo_ref, aux_ref, taps_ref, heads_ref,
    conv_ref, value_ref, scaled_ref, bc_ref, step_ref, cum_ref, cumt_ref, lead_ref, carry_ref,
    msg_ref, ext_ref, leadu_ref,
):
    tokens = z_ref.shape[0]
    width = halo_ref.shape[1]
    aux = aux_ref[...]
    ext_ref[0:8, :] = halo_ref[...]
    ext_ref[8 : 8 + tokens, :] = z_ref[:, :width]
    raw = z_ref[:, width : width + LANE] + heads_ref[0:1, :]
    step = jnp.maximum(raw, 0.0) + jnp.log1p(jnp.exp(-jnp.abs(raw)))
    rates = -step * jnp.exp(heads_ref[1:2, :])
    rows = lax.broadcasted_iota(jnp.int32, (tokens, tokens), 0)
    cols = lax.broadcasted_iota(jnp.int32, (tokens, tokens), 1)
    cum = dot_exact((rows >= cols).astype(F32), rates) * LOG2E
    lead = aux[:, 5:6] * jnp.exp2(cum[tokens - 1 : tokens, :] - cum)
    carry = aux[:, 4:5] * jnp.exp2(cum)
    step_ref[...] = step
    cum_ref[...] = cum
    cumt_ref[...] = cum.T
    lead_ref[...] = lead
    carry_ref[...] = carry
    lane_head = lane_heads(tokens, heads_tile)
    for q in range(width // LANE):
        at = tile_of(q)
        acc = taps_ref[4:5, at] + taps_ref[3:4, at] * z_ref[:, at]
        for j in range(3):
            acc = acc + taps_ref[j : j + 1, at] * (aux[:, j : j + 1] * ext_ref[5 + j : 5 + j + tokens, at])
        conv_ref[:, at] = acc
        value = acc * sigmoid(acc)
        if q < inner // LANE:
            value_ref[:, at] = value
            scaled = spread(step, q, heads_tile, lane_head) * value
            scaled_ref[:, at] = scaled.astype(BF16)
            leadu_ref[:, at] = (spread(lead, q, heads_tile, lane_head) * scaled).astype(BF16)
        else:
            base = q - inner // LANE
            bc_ref[:, tile_of(base)] = value.astype(BF16)
    state = dot_tn(bc_ref[:, :LANE], leadu_ref[...])
    msg_ref[0:LANE, :] = state.astype(BF16)
    msg_ref[LANE:, :] = jnp.zeros((SMALL_ROWS, inner), BF16)
    lane_row = lane_heads(1, heads_tile)
    for q in range(inner // LANE):
        through = spread(carry[tokens - 1 : tokens, :], q, heads_tile, lane_row)
        high, low = split_pair(through)
        msg_ref[LANE : LANE + 1, tile_of(q)] = high
        msg_ref[LANE + 1 : LANE + 2, tile_of(q)] = low


def intra_kernel(
    inner, heads_tile, scaled_ref, value_ref, bc_ref, cum_ref, cumt_ref, aux_ref, segt_ref, heads_ref,
    out_ref,
):
    tokens = scaled_ref.shape[0]
    scores = dot_nt(bc_ref[:, LANE:], bc_ref[:, :LANE])
    scores = jnp.where(tri_mask(tokens, aux_ref[:, 3:4], segt_ref[0:1, :], False), scores, 0.0)
    lane_head = lane_heads(tokens, heads_tile)
    lane_row = lane_heads(1, heads_tile)
    for q in range(inner // LANE):
        at = tile_of(q)
        total = spread(heads_ref[2:3, :], q, heads_tile, lane_row) * value_ref[:, at]
        scaled = scaled_ref[:, at]
        for i in range(heads_tile):
            h = q * heads_tile + i
            gap = jnp.minimum(cum_ref[:, h : h + 1] - cumt_ref[h : h + 1, :], 0.0)
            mixed = (jnp.exp2(gap) * scores).astype(BF16)
            total = total + jnp.where(lane_head == i, dot_nn(mixed, scaled), 0.0)
        out_ref[:, at] = total


def enter_states(messages):
    state = None
    for message in reversed(messages):
        own = message[0:LANE, :].astype(F32)
        through = message[LANE : LANE + 1, :].astype(F32) + message[LANE + 1 : LANE + 2, :].astype(F32)
        state = own if state is None else own + through * state
    return state


def gate_kernel(
    inner, heads_tile, count, with_grad, intra_ref, bc_ref, carry_ref, gate_ref, gain_ref, *refs
):
    messages = refs[:count]
    refs = refs[count:]
    if with_grad:
        branch_grad_ref, refs = refs[0], refs[1:]
    ssd_ref, state_ref, gated_ref, sums_ref = refs
    tokens = intra_ref.shape[0]
    state = enter_states([m[...] for m in messages]).astype(BF16)
    state_ref[...] = state
    inter = dot_nn(bc_ref[:, LANE:], state)
    lane_head = lane_heads(tokens, heads_tile)
    carry = carry_ref[...]
    squares = jnp.zeros((tokens, LANE), F32)
    products = jnp.zeros((tokens, LANE), F32)
    for q in range(inner // LANE):
        at = tile_of(q)
        ssd = intra_ref[:, at] + spread(carry, q, heads_tile, lane_head) * inter[:, at]
        ssd_ref[:, at] = ssd
        gate = gate_ref[:, at]
        gated = ssd * (gate * sigmoid(gate))
        squares = squares + gated * gated
        scaled = gated * gain_ref[0:1, at]
        gated_ref[:, at] = scaled.astype(BF16)
        if with_grad:
            products = products + scaled * branch_grad_ref[:, at]
    total = jnp.sum(squares, axis=1, keepdims=True)
    lanes = lax.broadcasted_iota(jnp.int32, (tokens, LANE), 1)
    packed = jnp.where(lanes == 0, total, 0.0)
    if with_grad:
        packed = packed + jnp.where(lanes == 1, jnp.sum(products, axis=1, keepdims=True), 0.0)
        sums_ref[...] = packed.T[0:8, :]
    else:
        sums_ref[...] = packed


def ungate_kernel(
    inner, heads_tile, norm_width, branch_grad_ref, norm_ref, gate_ref, ssd_ref, gain_ref, carry_ref, bc_ref,
    gssd_ref, ggate_ref, branch_ref, msg_ref, ggain_ref, cg_ref,
):
    tokens = branch_grad_ref.shape[0]
    rho = norm_ref[:, 0:1]
    pull = norm_ref[:, 1:2] * (rho * rho * rho / norm_width)
    lane_head = lane_heads(tokens, heads_tile)
    carry = carry_ref[...]
    ggain_ref[...] = jnp.zeros(ggain_ref.shape, F32)
    for q in range(inner // LANE):
        at = tile_of(q)
        gate = gate_ref[:, at]
        sig = sigmoid(gate)
        ssd = ssd_ref[:, at]
        gated = ssd * (gate * sig)
        grad = branch_grad_ref[:, at]
        gain = gain_ref[0:1, at]
        normed = gated * rho
        ggain_ref[0:1, at] = jnp.sum(grad * normed, axis=0, keepdims=True)
        branch_ref[:, at] = (normed * gain).astype(BF16)
        ggated = rho * (gain * grad) - gated * pull
        gssd = ggated * (gate * sig)
        gssd_ref[:, at] = gssd
        ggate_ref[:, at] = (ggated * ssd * (sig * (1.0 + gate * (1.0 - sig)))).astype(BF16)
        cg_ref[:, at] = (spread(carry, q, heads_tile, lane_head) * gssd).astype(BF16)
    msg_ref[0:LANE, :] = dot_tn(bc_ref[:, LANE:], cg_ref[...]).astype(BF16)
    msg_ref[LANE:, :] = jnp.zeros((SMALL_ROWS, inner), BF16)
    lane_row = lane_heads(1, heads_tile)
    for q in range(inner // LANE):
        through = spread(carry[tokens - 1 : tokens, :], q, heads_tile, lane_row)
        high, low = split_pair(through)
        msg_ref[LANE : LANE + 1, tile_of(q)] = high
        msg_ref[LANE + 1 : LANE + 2, tile_of(q)] = low


def intra_grad_kernel(
    inner, heads_tile, scaled_ref, gssd_ref, bc_ref, cum_ref, cumt_ref, aux_ref, segt_ref,
    gscaled_ref, gbc_ref, gcum_ref, sums_ref,
):
    tokens = scaled_ref.shape[0]
    mask = tri_mask(tokens, aux_ref[:, 3:4], segt_ref[0:1, :], True)
    scores = jnp.where(mask, dot_nt(bc_ref[:, :LANE], bc_ref[:, LANE:]), 0.0)
    lane_head = lane_heads(tokens, heads_tile)
    gscores = jnp.zeros((tokens, tokens), F32)
    gcum_ref[...] = jnp.zeros(gcum_ref.shape, F32)
    sums_ref[...] = jnp.zeros(sums_ref.shape, F32)
    for q in range(inner // LANE):
        at = tile_of(q)
        grad = gssd_ref[:, at].astype(BF16)
        scaled = scaled_ref[:, at]
        total = jnp.zeros((tokens, LANE), F32)
        for i in range(heads_tile):
            h = q * heads_tile + i
            gap = jnp.minimum(cumt_ref[h : h + 1, :] - cum_ref[:, h : h + 1], 0.0)
            decay = jnp.exp2(gap)
            mixed = decay * scores
            picked = jnp.where(lane_head == i, scaled, jnp.zeros_like(scaled))
            gmixed = dot_nt(picked, grad)
            total = total + jnp.where(lane_head == i, dot_nn(mixed.astype(BF16), grad), 0.0)
            product = gmixed * mixed
            sums_ref[h : h + 1, :] = jnp.sum(product, axis=0, keepdims=True)
            gcum_ref[:, h : h + 1] = -jnp.sum(product, axis=1, keepdims=True)
            gscores = gscores + gmixed * decay
        gscaled_ref[:, at] = total
    gscores = jnp.where(mask, gscores, 0.0)
    gbc_ref[:, :LANE] = dot_nn(gscores.astype(BF16), bc_ref[:, LANE:])
    gbc_ref[:, LANE:] = dot_nn(gscores.T.astype(BF16), bc_ref[:, :LANE])
    gcum_ref[...] = gcum_ref[...] + sums_ref[...].T


def inter_grad_kernel(
    inner, heads_tile, count, state_ref, scaled_ref, value_ref, gssd_ref, gscaled_ref, bc_ref, gbc_ref, gcum_ref,
    step_ref, lead_ref, carry_ref, z_ref, halo_ref, conv_ref, aux_ref, taps_ref, heads_ref, pick_ref, *refs,
):
    messages = refs[:count]
    (
        gpre_ref, gstep_ref, gtaps_ref, gheads_ref,
        ext_ref, em_ref, leadu_ref, cg_ref, gain_ref, lose_ref, gsize_ref,
    ) = refs[count:]
    tokens = scaled_ref.shape[0]
    width = halo_ref.shape[1]
    aux = aux_ref[...]
    adjoint = enter_states([m[...] for m in messages])
    adjoint_low = adjoint.astype(BF16)
    state = state_ref[...]
    from_adjoint = dot_nn(bc_ref[:, :LANE], adjoint_low)
    from_state = dot_nn(bc_ref[:, LANE:], state)
    overlap = jnp.sum(adjoint * state.astype(F32), axis=0, keepdims=True)
    lane_head = lane_heads(tokens, heads_tile)
    lane_row = lane_heads(1, heads_tile)
    step = step_ref[...]
    lead = lead_ref[...]
    carry = carry_ref[...]
    ext_ref[0:8, :] = halo_ref[...]
    ext_ref[8 : 8 + tokens, :] = z_ref[:, :width]
    em_ref[0:8, :] = jnp.zeros((8, LANE), F32)
    em_ref[8 + tokens :, :] = jnp.zeros((8, LANE), F32)
    gtaps_ref[...] = jnp.zeros(gtaps_ref.shape, F32)
    gheads_ref[...] = jnp.zeros(gheads_ref.shape, F32)

    def through_conv(q, grad):
        at = tile_of(q)
        conv = conv_ref[:, at]
        sig = sigmoid(conv)
        e = grad * (sig * (1.0 + conv * (1.0 - sig)))
        gtaps_ref[4:5, at] = jnp.sum(e, axis=0, keepdims=True)
        gtaps_ref[3:4, at] = jnp.sum(e * z_ref[:, at], axis=0, keepdims=True)
        total = None
        for j in range(3):
            masked = aux[:, j : j + 1] * e
            gtaps_ref[j : j + 1, at] = jnp.sum(masked * ext_ref[5 + j : 5 + j + tokens, at], axis=0, keepdims=True)
            em_ref[8 : 8 + tokens, :] = masked
            term = taps_ref[j : j + 1, at] * em_ref[3 - j : 11 - j + tokens, :]
            total = term if total is None else total + term
        gpre_ref[0:8, at] = total[0:8, :]
        gpre_ref[8:, at] = total[8:, :] + taps_ref[3:4, at] * e

    for q in range(inner // LANE):
        at = tile_of(q)
        scaled = scaled_ref[:, at].astype(F32)
        grad = gssd_ref[:, at]
        value = value_ref[:, at]
        leads = spread(lead, q, heads_tile, lane_head)
        carries = spread(carry, q, heads_tile, lane_head)
        pushed = leads * from_adjoint[:, at]
        gscaled = gscaled_ref[:, at] + pushed
        carried = carries * grad
        leadu_ref[:, at] = (leads * scaled).astype(BF16)
        cg_ref[:, at] = carried.astype(BF16)
        gain_ref[:, at] = (carried * from_state[:, at]).astype(BF16)
        lose_ref[:, at] = (scaled * pushed).astype(BF16)
        gsize_ref[:, at] = (gscaled * value).astype(BF16)
        gtaps_ref[5:6, at] = jnp.sum(grad * value, axis=0, keepdims=True)
        gvalue = spread(step, q, heads_tile, lane_head) * gscaled
        gvalue = gvalue + spread(heads_ref[2:3, :], q, heads_tile, lane_row) * grad
        through_conv(q, gvalue)
    gb = gbc_ref[:, :LANE] + dot_nt(leadu_ref[...], adjoint_low)
    gc = gbc_ref[:, LANE:] + dot_nt(cg_ref[...], state)
    through_conv(inner // LANE, gb)
    through_conv(inner // LANE + 1, gc)
    pick = pick_ref[...]
    lose = dot_nn(lose_ref[...], pick)
    gcum = gcum_ref[...] + dot_nn(gain_ref[...], pick) - lose
    high, low = split_pair(overlap)
    ends = dot_nn(jnp.broadcast_to(high, (8, inner)), pick) + dot_nn(jnp.broadcast_to(low, (8, inner)), pick)
    last = carry[tokens - 1 : tokens, :] * ends[0:1, :] + jnp.sum(lose, axis=0, keepdims=True)
    row_of = lax.broadcasted_iota(jnp.int32, (tokens, LANE), 0)
    gcum = gcum + jnp.where(row_of == tokens - 1, last, 0.0)
    rows = lax.broadcasted_iota(jnp.int32, (tokens, tokens), 0)
    cols = lax.broadcasted_iota(jnp.int32, (tokens, tokens), 1)
    grate = dot_exact((rows <= cols).astype(F32), gcum)
    speed = jnp.exp(heads_ref[1:2, :])
    gsize = dot_nn(gsize_ref[...], pick) - speed * grate
    raw = z_ref[:, width : width + LANE] + heads_ref[0:1, :]
    graw = gsize * sigmoid(raw)
    gstep_ref[...] = graw.astype(BF16)
    gheads_ref[0:1, :] = jnp.sum(graw, axis=0, keepdims=True)
    gheads_ref[1:2, :] = jnp.sum(grate * (-speed * step), axis=0, keepdims=True)


def permute(block, axis, route):
    return lax.ppermute(block, axis, route)


def from_before(block, count, distance):
    return permute(block, "row", [(i, i + distance) for i in range(count - distance)])


def from_after(block, count, distance):
    return permute(block, "row", [(i + distance, i) for i in range(count - distance)])


def swapped(block):
    return permute(block, "pipe", [(0, 1), (1, 0)])


def col_sum(block):
    count = lax.axis_size("col")
    rows = block.shape[0] // count
    parts = lax.all_to_all(block.reshape(count, rows, block.shape[1]), "col", 0, 0)
    own = jnp.sum(parts.astype(F32), axis=0)
    return own


def col_gather(block):
    return lax.all_gather(block, "col", axis=0, tiled=True)


def local(
    inputs, cotangent, segment_ids, batch_order, norm_gain, gate_proj, value_proj, step_proj, state_proj,
    conv_value, conv_value_bias, conv_state, conv_state_bias, step_bias, decay_log, skip_gain, gate_gain, out_proj,
):
    core = lax.axis_index("pipe")
    first = core == 0
    rows = lax.axis_size("row")
    row = lax.axis_index("row")
    tokens, width = inputs.shape[1], inputs.shape[2]
    shard = gate_proj.shape[1]
    inner = gate_proj.shape[2]
    heads = step_proj.shape[2]
    states = state_proj.shape[2] // 2
    heads_tile = LANE // (inner // heads)
    half = inner // 2
    conv_width = inner + 2 * states
    norm_width = inner * lax.axis_size("col")
    distances = range(1, rows)

    def pick_mine(a, b):
        return jnp.where(first, a, b)

    step_pad = jnp.pad(step_proj[0], ((0, 0), (0, LANE - heads)))
    out_t = out_proj[0].T
    packs_a = [
        jnp.concatenate(
            [value_proj[0][:, i * half : (i + 1) * half], state_proj[0][:, i * states : (i + 1) * states], step_pad],
            axis=1,
        )
        for i in range(2)
    ]
    packs_b = [
        jnp.concatenate([gate_proj[0][:, i * half : (i + 1) * half], out_t[:, i * half : (i + 1) * half]], axis=1)
        for i in range(2)
    ]
    keep_a, give_a = pick_mine(packs_a[0], packs_a[1]), pick_mine(packs_a[1], packs_a[0])
    keep_b, give_b = pick_mine(packs_b[0], packs_b[1]), pick_mine(packs_b[1], packs_b[0])
    take_a, take_b = swapped(give_a), swapped(give_b)
    gather = functools.partial(lax.all_gather, axis_name="row", axis=0, tiled=True)
    mine_a = [gather(pick_mine(keep_a, take_a))]
    mine_b = [gather(pick_mine(keep_b, take_b))]
    mine_a.append(gather(pick_mine(take_a, keep_a)))
    mine_b.append(gather(pick_mine(take_b, keep_b)))
    other_a = [swapped(w) for w in mine_a]
    other_b = [swapped(w) for w in mine_b]

    small = jnp.concatenate(
        [
            v.reshape(-1)
            for v in (norm_gain, conv_value, conv_value_bias, conv_state, conv_state_bias, step_bias, decay_log, skip_gain, gate_gain)
        ]
    )
    small_other = swapped(small)
    smalls = (pick_mine(small, small_other), pick_mine(small_other, small))

    def unpack(vector):
        out, at = [], 0
        for v in (norm_gain, conv_value, conv_value_bias, conv_state, conv_state_bias, step_bias, decay_log, skip_gain, gate_gain):
            out.append(vector[at : at + v.size].reshape(v.shape[1:]))
            at += v.size
        gain_in, cvw, cvb, csw, csb, sbias, dlog, skip, gain_out = out
        taps = jnp.concatenate(
            [jnp.concatenate([cvw, csw], axis=1), jnp.concatenate([cvb, csb])[None], jnp.zeros((3, conv_width), F32)], axis=0
        )
        head_rows = jnp.pad(jnp.stack([sbias, dlog, skip]), ((0, 5), (0, LANE - heads)))
        return gain_in, taps, head_rows, gain_out[None]

    params = [unpack(v) for v in smalls]

    source = batch_order[core]
    layer_in = inputs[source]
    seg = segment_ids[source].astype(F32)
    seg_before = from_before(seg[-3:], rows, 1)
    seg_before = jnp.where(row == 0, -1.0, seg_before)
    seg_ext = jnp.concatenate([seg_before, seg])
    same = [(seg_ext[j : j + tokens] == seg).astype(F32) for j in range(3)]
    carry_mask = (seg == seg_before[2]).astype(F32)
    inside = (seg == seg[tokens - 1]).astype(F32)
    aux = jnp.pad(jnp.stack(same + [seg, carry_mask, inside], axis=1), ((0, 0), (0, LANE - 6)))
    seg_t = jnp.broadcast_to(seg[None], (8, tokens))
    pick = (
        (lax.broadcasted_iota(jnp.int32, (inner, LANE), 0) // (inner // heads))
        == lax.broadcasted_iota(jnp.int32, (inner, LANE), 1)
    ).astype(BF16)

    prep = on_chip(
        functools.partial(prep_kernel, inner, heads_tile),
        (
            shaped((tokens, conv_width)), shaped((tokens, inner)), shaped((tokens, inner), BF16),
            shaped((tokens, 2 * states), BF16), shaped((tokens, LANE)), shaped((tokens, LANE)), shaped((LANE, tokens)),
            shaped((tokens, LANE)), shaped((tokens, LANE)), shaped((states + SMALL_ROWS, inner), BF16),
        ),
        [pltpu.VMEM((tokens + 8, conv_width), F32), pltpu.VMEM((tokens, inner), BF16)],
    )
    intra = on_chip(functools.partial(intra_kernel, inner, heads_tile), shaped((tokens, inner)))
    gate_outs = (shaped((tokens, inner)), shaped((states, inner), BF16), shaped((tokens, inner), BF16))
    gates = [
        on_chip(
            functools.partial(gate_kernel, inner, heads_tile, rows - 1, with_grad),
            gate_outs + (shaped((8, tokens)) if with_grad else shaped((tokens, LANE)),),
        )
        for with_grad in (False, True)
    ]
    ungate = on_chip(
        functools.partial(ungate_kernel, inner, heads_tile, norm_width),
        (
            shaped((tokens, inner)), shaped((tokens, inner), BF16), shaped((tokens, inner), BF16),
            shaped((states + SMALL_ROWS, inner), BF16), shaped((8, inner)),
        ),
        [pltpu.VMEM((tokens, inner), BF16)],
    )
    intra_grad = on_chip(
        functools.partial(intra_grad_kernel, inner, heads_tile),
        (shaped((tokens, inner)), shaped((tokens, 2 * states)), shaped((tokens, LANE))),
        [pltpu.VMEM((LANE, tokens), F32)],
    )
    inter_grad = on_chip(
        functools.partial(inter_grad_kernel, inner, heads_tile, rows - 1),
        (
            shaped((tokens + 8, conv_width)), shaped((tokens, LANE), BF16), shaped((8, conv_width)), shaped((8, LANE)),
        ),
        [pltpu.VMEM((tokens + 8, conv_width), F32), pltpu.VMEM((tokens + 16, LANE), F32)]
        + [pltpu.VMEM((tokens, inner), BF16)] * 5,
    )

    def halves(a):
        return a[:, :half], a[:, half:]

    def joined(mine, other):
        return jnp.where(first, jnp.concatenate([mine, other], 1), jnp.concatenate([other, mine], 1))

    def project(layer, x):
        gain_in = params[layer][0]
        xf = x.astype(F32)
        scale = lax.rsqrt(jnp.mean(xf * xf, axis=-1, keepdims=True) + EPSILON)
        normed = (xf * scale * gain_in[None]).astype(BF16)
        za_mine = dot_nn(normed, mine_a[layer])
        za_other = dot_nn(normed, other_a[layer])
        z = jnp.concatenate(
            [
                joined(za_mine[:, :half], za_other[:, :half]),
                joined(za_mine[:, half : half + states], za_other[:, half : half + states]),
                za_mine[:, half + states :],
            ],
            axis=1,
        )
        halo = jnp.pad(from_before(z[tokens - 3 :, :conv_width], rows, 1), ((5, 0), (0, 0)))
        gate = joined(dot_nn(normed, mine_b[layer][:, :half]), dot_nn(normed, other_b[layer][:, :half]))
        return scale, normed, z, halo, gate

    def scan_part(layer, z, halo):
        taps, head_rows = params[layer][1:3]
        made = prep(z, halo, aux, taps, head_rows)
        conv, value, scaled, bc, step, cum, cumt, lead, carry, message = made
        messages = [from_before(message, rows, d) for d in distances]
        inside_part = intra(scaled, value, bc, cum, cumt, aux, seg_t, head_rows)
        return made, messages, inside_part

    def out_product(layer, gated):
        low, high = halves(gated)
        mine, other = pick_mine(low, high), pick_mine(high, low)
        return dot_nt(mine, mine_b[layer][:, half:]) + dot_nt(other, other_b[layer][:, half:])

    def branch_grad_of(layer, g_out):
        return joined(dot_nn(g_out, mine_b[layer][:, half:]), dot_nn(g_out, other_b[layer][:, half:]))

    scale0, normed0, z0, halo0, gate0 = project(0, layer_in)
    made0, messages0, inside0 = scan_part(0, z0, halo0)
    ssd0, state0, gated0, sums0 = gates[0](inside0, made0[3], made0[8], gate0, params[0][3], *messages0)
    partial0 = out_product(0, gated0)
    square_high, square_low = split_pair(sums0[:, :1])
    lanes_pad = jnp.zeros((tokens, LANE - 2), BF16)
    own0 = col_sum(jnp.concatenate([partial0.astype(BF16), square_high, square_low, lanes_pad], axis=1))
    own_square = own0[:, width : width + 1] + own0[:, width + 1 : width + 2]
    own_high, own_low = split_pair(own_square)
    full0 = col_gather(
        jnp.concatenate([own0[:, :width].astype(BF16), own_high, own_low, lanes_pad[: own_high.shape[0]]], axis=1)
    )
    raw0 = full0[:, :width].astype(F32)
    rho0 = lax.rsqrt(
        (full0[:, width : width + 1].astype(F32) + full0[:, width + 1 : width + 2].astype(F32)) / norm_width + EPSILON
    )
    x1 = (layer_in.astype(F32) + rho0 * raw0).astype(BF16)

    g_out1 = cotangent[core]
    scale1, normed1, z1, halo1, gate1 = project(1, x1)
    made1, messages1, inside1 = scan_part(1, z1, halo1)
    gbranch1 = branch_grad_of(1, g_out1)
    ssd1, state1, gated1, sums1 = gates[1](inside1, made1[3], made1[8], gate1, params[1][3], *messages1, gbranch1)
    totals1 = jnp.sum(lax.all_gather(sums1[0:8], "col"), axis=0)
    rho1 = lax.rsqrt(totals1[0] / norm_width + EPSILON)[:, None]
    norm1 = jnp.pad(jnp.concatenate([rho1, totals1[1][:, None]], axis=1), ((0, 0), (0, LANE - 2)))
    partial1 = out_product(1, gated1).astype(BF16)
    raw1 = lax.psum(partial1, "col")
    x2 = (x1.astype(F32) + rho1 * raw1.astype(F32)).astype(BF16)

    def backward(layer, x, g_sum, g_out, gbranch, norm, scale, normed, z, halo, gate, made, ssd, state):
        conv, value, scaled, bc, step, cum, cumt, lead, carry, _ = made
        gain_in, taps, head_rows, gain_out = params[layer]
        gssd, ggate, branch, message, ggain = ungate(gbranch, norm, gate, ssd, gain_out, carry, bc)
        messages = [from_after(message, rows, d) for d in distances]
        gscaled, gbc, gcum = intra_grad(scaled, gssd, bc, cum, cumt, aux, seg_t)
        gpre, gstep, gtaps, gheads = inter_grad(
            state, scaled, value, gssd, gscaled, bc, gbc, gcum, step, lead, carry, z, halo, conv, aux, taps, head_rows,
            pick, *messages,
        )
        from_next = from_after(gpre[5:8], rows, 1)
        gpre = jnp.concatenate([gpre[8 : tokens + 5], gpre[tokens + 5 :] + from_next], axis=0)
        glow = gpre.astype(BF16)
        v_low, v_high = halves(glow[:, :inner])
        s_low, s_high = glow[:, inner : inner + states], glow[:, inner + states :]
        ga_mine = jnp.concatenate([pick_mine(v_low, v_high), pick_mine(s_low, s_high)], axis=1)
        ga_other = jnp.concatenate([pick_mine(v_high, v_low), pick_mine(s_high, s_low)], axis=1)
        g_low, g_high = halves(ggate)
        gg_mine, gg_other = pick_mine(g_low, g_high), pick_mine(g_high, g_low)
        b_low, b_high = halves(branch)
        br_mine, br_other = pick_mine(b_low, b_high), pick_mine(b_high, b_low)
        ga_full = jnp.concatenate([ga_mine, gstep], axis=1)
        partial = dot_nt(ga_full, mine_a[layer]) + dot_nt(ga_other, other_a[layer][:, : half + states])
        partial = partial + dot_nt(gg_mine, mine_b[layer][:, :half]) + dot_nt(gg_other, other_b[layer][:, :half])
        own = col_sum(jnp.concatenate([partial.astype(BF16), glow[:, inner:]], axis=1))
        full = col_gather(own.astype(BF16))
        gnormed = full[:, :width].astype(F32)
        state_low = full[:, width:]
        xf = x.astype(F32)
        ggx = gnormed * gain_in[None]
        pull = jnp.sum(ggx * xf, axis=1, keepdims=True) * (scale * scale * scale / width)
        g_in = g_sum + scale * ggx - xf * pull
        ggain_in = jnp.sum(gnormed * xf * scale, axis=0)
        st_low, st_high = state_low[:, :states], state_low[:, states:]
        dw_b = [
            jnp.concatenate([dot_tn(normed, a), dot_tn(g_out, b)], axis=1).astype(BF16)
            for a, b in ((gg_mine, br_mine), (gg_other, br_other))
        ]
        dw_a = [
            dot_tn(normed, jnp.concatenate([v, s, gstep], axis=1)).astype(BF16)
            for v, s in (
                (pick_mine(v_low, v_high), pick_mine(st_low, st_high)),
                (pick_mine(v_high, v_low), pick_mine(st_high, st_low)),
            )
        ]

        def reduced(pair):
            both = (pair[0].astype(F32) + swapped(pair[1]).astype(F32)).astype(BF16)
            return lax.psum_scatter(both, "row", scatter_dimension=0, tiled=True)

        shares = (reduced(dw_a), reduced(dw_b))
        terms = (ggain_in, gtaps, gheads, ggain)
        return g_in, shares, terms

    g_sum1 = g_out1.astype(F32)
    g_in1, shares1, terms1 = backward(
        1, x1, g_sum1, g_out1, gbranch1, norm1, scale1, normed1, z1, halo1, gate1, made1, ssd1, state1
    )
    g_out0 = g_in1.astype(BF16)
    dots0 = jnp.sum(g_out0.astype(F32) * raw0, axis=1, keepdims=True)
    norm0 = jnp.pad(jnp.concatenate([rho0, dots0], axis=1), ((0, 0), (0, LANE - 2)))
    gbranch0 = branch_grad_of(0, g_out0)
    g_in0, shares0, terms0 = backward(
        0, layer_in, g_out0.astype(F32), g_out0, gbranch0, norm0, scale0, normed0, z0, halo0, gate0, made0, ssd0, state0
    )

    def small_vector(terms):
        ggain_in, gtaps, gheads, ggain = terms
        skip = gtaps[5, :inner].reshape(heads, inner // heads).sum(axis=1)
        own = [ggain_in, gtaps[:4, :inner], gtaps[4, :inner], gheads[0, :heads], gheads[1, :heads], skip, ggain[0]]
        return jnp.concatenate([v.reshape(-1) for v in own]), jnp.concatenate([gtaps[:4, inner:].reshape(-1), gtaps[4, inner:]])

    (own0_vec, part0), (own1_vec, part1) = small_vector(terms0), small_vector(terms1)
    own_sum = lax.psum(jnp.stack([own0_vec, own1_vec]), ("pipe", "row"))
    part_sum = lax.psum(jnp.stack([part0, part1]), ("pipe", "row", "col"))
    own_sum = pick_mine(own_sum[0], own_sum[1])
    part_sum = pick_mine(part_sum[0], part_sum[1])

    def cut(vector, sizes):
        out, at = [], 0
        for size in sizes:
            out.append(vector[at : at + size])
            at += size
        return out

    s_gain, s_cv, s_cvb, s_sb, s_dl, s_sk, s_gg = cut(own_sum, (width, 4 * inner, inner, heads, heads, heads, inner))
    s_cs, s_csb = cut(part_sum, (8 * states, 2 * states))

    def settled(index):
        mine = pick_mine(shares0[index], shares1[index])
        other = swapped(pick_mine(shares1[index], shares0[index]))
        low, high = pick_mine(mine, other).astype(F32), pick_mine(other, mine).astype(F32)
        return low, high

    a_low, a_high = settled(0)
    b_low, b_high = settled(1)
    d_value = jnp.concatenate([a_low[:, :half], a_high[:, :half]], axis=1)
    d_state = jnp.concatenate([a_low[:, half : half + states], a_high[:, half : half + states]], axis=1)
    d_step = a_low[:, half + states : half + states + heads]
    d_gate = jnp.concatenate([b_low[:, :half], b_high[:, :half]], axis=1)
    d_out = jnp.concatenate([b_low[:, half:], b_high[:, half:]], axis=1).T

    mine_out, give_out = pick_mine(x1, x2), pick_mine(x2, x1)
    take_out = swapped(give_out)
    layer_outputs = jnp.stack([pick_mine(mine_out, take_out), pick_mine(take_out, mine_out)])
    mine_grad, give_grad = pick_mine(g_in0, g_in1), pick_mine(g_in1, g_in0)
    take_grad = swapped(give_grad)
    by_batch = (pick_mine(mine_grad, take_grad), pick_mine(take_grad, mine_grad))
    flipped = first & (batch_order[0] == 1)
    input_grads = jnp.stack([jnp.where(flipped, by_batch[1], by_batch[0]), jnp.where(flipped, by_batch[0], by_batch[1])])

    return (
        layer_outputs[None],
        input_grads[None],
        s_gain[None],
        d_gate[None],
        d_value[None],
        d_step[None],
        d_state[None],
        s_cv.reshape(1, 4, inner),
        s_cvb[None],
        s_cs.reshape(1, 4, 2 * states),
        s_csb[None],
        s_sb[None],
        s_dl[None],
        s_sk[None],
        s_gg[None],
        d_out[None],
    )


def solution(mesh):
    in_specs = (
        P(None, "row", None),
        P(None, "row", None),
        P(None, "row"),
        P(),
        P("pipe", None),
        P("pipe", "row", "col"),
        P("pipe", "row", "col"),
        P("pipe", "row", "col"),
        P("pipe", "row", None),
        P("pipe", None, "col"),
        P("pipe", "col"),
        P("pipe", None, None),
        P("pipe", None),
        P("pipe", "col"),
        P("pipe", "col"),
        P("pipe", "col"),
        P("pipe", "col"),
        P("pipe", "col", "row"),
    )
    out_specs = (
        P("pipe", None, "row", None),
        P("pipe", None, "row", None),
        P("pipe", None),
        P("pipe", "row", "col"),
        P("pipe", "row", "col"),
        P("pipe", "row", "col"),
        P("pipe", "row", None),
        P("pipe", None, "col"),
        P("pipe", "col"),
        P("pipe", None, None),
        P("pipe", None),
        P("pipe", "col"),
        P("pipe", "col"),
        P("pipe", "col"),
        P("pipe", "col"),
        P("pipe", "col", "row"),
    )
    return jax.shard_map(local, mesh=mesh, in_specs=in_specs, out_specs=out_specs, check_vma=False)
```

time: 1730 us -> 628 us (0.36)
  waiting for transfers between devices: 756 us -> 136 us
  matrix products: 278 us -> 73.9 us
  blocking collectives: 287 us -> 173 us
  other arithmetic: 145 us -> 61.1 us
  local copies, waits for them, and re-layouts: 104 us -> 49.3 us
  Pallas kernels: 0 us -> 54.2 us
  loops' own time: 53.4 us -> 0 us
  starting transfers between devices: 77.9 us -> 51.5 us
    psum x6 -> x1, waiting for transfers between devices: 315 us -> 0.02 us  [local(): raw1 = lax.psum(partial1, 'col')]
    reduce_scatter x5 -> x2, waiting for transfers between devices: 207 us -> 0.01 us  [reduced(): return lax.psum_scatter(both, 'row', scatter_dimension=0, tiled=True)]
    dot_general x117 -> x36, matrix products: 278 us -> 73.9 us  [the longest x12 27.4 us: dot_tn(): lax.dot_general(a, b, (((0,), (0,)), ((), ())), preferred_element_type=F32)]
    psum x13 -> x2, blocking collectives: 222 us -> 67.7 us  [the longest x1 37.9 us: local(): part_sum = lax.psum(jnp.stack([part0, part1]), ('pipe', 'row', 'col'))]
    all_gather x12 -> x4, waiting for transfers between devices: 220 us -> 93.3 us  [the longest x1 39 us: local(): mine_b = [gather(pick_mine(keep_b, take_b))]]
    pallas_call x0 -> x12, Pallas kernels: none -> 54.2 us  [call(): pl.pallas_call(kernel, out_shape=out_shapes, in_specs=[whole] * len(opera...]
    another operation x11 -> x0, loops' own time: 53.4 us -> none  [the longest x1 40.2 us: local(): lax.scan(backward_step, (zero_rows, full_zero, small_zero), jnp.arange(st...]
    reduce_sum x27 -> x11, other arithmetic: 42.5 us -> 6.6 us  [the longest x2 2.81 us: backward(): ggain_in = jnp.sum(gnormed * xf * scale, axis=0)]
  transfers between devices with their start and end apart: 53 -> 43, of which waited for: 32 -> 14; matrix products, arithmetic and copies ran while one was open for 15% -> 26% of each run, Pallas kernels for 0% -> 6%
where the time goes in v1:
time: 628 us; the launch traced here: 617 us
  blocking collectives  173 us (28%)
  waiting for transfers between devices  136 us (22%)
  matrix products  73.9 us (12%)
  other arithmetic  61.1 us (10%)
  Pallas kernels  54.2 us (9%)
  starting transfers between devices  51.5 us (8%)
  local copies, waits for them, and re-layouts  49.3 us (8%)
  between operations  18.7 us (3%)
    all_gather x3, blocking collectives, col_gather(): return lax.all_gather(block, 'col', axis=0, tiled=True)  66.8 us
    pallas_call x12, Pallas kernels, call(): pl.pallas_call(kernel, out_shape=out_shapes, in_specs=[whole] * len(opera...  54.2 us
    ppermute x32, starting transfers between devices, permute(): return lax.ppermute(block, axis, route)  42.2 us
    all_gather x1, waiting for transfers between devices, local(): mine_b = [gather(pick_mine(keep_b, take_b))]  39 us
    psum x1, blocking collectives, local(): part_sum = lax.psum(jnp.stack([part0, part1]), ('pipe', 'row', 'col'))  37.9 us
    all_gather x1, waiting for transfers between devices, local(): mine_b.append(gather(pick_mine(take_b, keep_b)))  35 us
    psum x1, blocking collectives, local(): own_sum = lax.psum(jnp.stack([own0_vec, own1_vec]), ('pipe', 'row'))  29.7 us
    dot_general x12, matrix products, dot_tn(): lax.dot_general(a, b, (((0,), (0,)), ((), ())), preferred_element_type=F32)  27.4 us
  transfers between devices with their start and end apart: 43, of which 14 were waited for; matrix products, arithmetic and copies ran while one was open for 26% of the time, Pallas kernels for 6%

profile of v1, /device:TPU:0, one launch (start us, length us, event | category | flops | bytes accessed | tf_op | source)
XLA Modules:
  0.0 617.3 jit_solution(8757495611058875669)
XLA Ops:
  21.7 4.5 collective-permute-start.4
  30.6 19.3 %all-gather.6.cloned.1.call-done = bf16[1536,640]{1,0:T(8,128)(2,1)} async-done(((bf16[384,640]{1,0:T(8,128)(2,1)}), bf16[1536,640]{1,0:T(8,128)(2,1)}) %all-gather.6.cloned.1.call-update) | async-done | bytes 1966096 | tf_op jit(solution)/shard_map/all_gather | solution.py:435
  50.6 39.0 %all-gather.8.cloned.1.call-done = bf16[1536,768]{0,1:T(8,128)(2,1)} async-done(((bf16[384,768]{0,1:T(8,128)(2,1)}), bf16[1536,768]{0,1:T(8,128)(2,1)}) %all-gather.8.cloned.1.call-update) | async-done | bytes 2359312 | tf_op jit(solution)/shard_map/all_gather | solution.py:436
  94.4 35.0 %all-gather.12.cloned.1.call-done = bf16[1536,768]{0,1:T(8,128)(2,1)} async-done(((bf16[384,768]{0,1:T(8,128)(2,1)}), bf16[1536,768]{0,1:T(8,128)(2,1)}) %all-gather.12.cloned.1.call-update) | async-done | bytes 2359312 | tf_op jit(solution)/shard_map/all_gather | solution.py:438
  157.4 4.9 collective-permute-done.8.refs_1_
  171.2 4.6 all-to-all-start
  183.6 13.7 %all-to-all-done = bf16[4,64,1664]{2,1,0:T(8,128)(2,1)S(1)} async-done(((bf16[4,64,1664]{2,1,0:T(8,128)(2,1)}), bf16[4,64,1664]{2,1,0:T(8,128)(2,1)S(1)}, u32[]{:S(2)}, u32[]{:S(2)}) %all-to-all-start) | async-done | bytes 852000 | tf_op jit(solution)/shard_map/all_to_all | solution.py:387
  197.7 18.4 %all_gather.29 = bf16[256,1664]{1,0:T(8,128)(2,1)S(1)} all-gather(bf16[64,1664]{1,0:T(8,128)(2,1)S(1)} %concatenate.204), channel_id=1, replica_groups=mesh['pipe'=2,'row'=4,'col'=4] {'col'}, dimensions={0}, use_global_device_ids=true | all-gather | bytes 1064960 | tf_op jit(solution)/shard_map/all_gather | solution.py:393
  229.0 6.6 %collective-permute-start.13 = (bf16[144,768]{1,0:T(8,128)(2,1)}, bf16[144,768]{1,0:T(8,128)(2,1)S(1)}, u32[]{:S(2)}, u32[]{:S(2)}) collective-permute-start(bf16[144,768]{1,0:T(8,128)(2,1)} %get-tuple-element.83), channel_id=1, source_target_pairs={{0,4},{4,8},{8,12},{1,5},{5,9},{9,13},{2,6},{6,10},{10,14},{3,7},{... | collective-permute-start | bytes 663560 | tf_op jit(solution)/shard_map/ppermute | solution.py:369
  250.8 13.3 %all-gather = f32[32,256]{1,0:T(8,128)S(1)} all-gather(f32[8,256]{1,0:T(8,128)} %get-tuple-element.84), channel_id=2, replica_groups=mesh['pipe'=2,'row'=4,'col'=4] {'col'}, dimensions={0}, use_global_device_ids=true | all-gather | bytes 40960 | tf_op jit(solution)/shard_map/all_gather | solution.py:585
  273.4 4.9 shard_map.304
  286.8 7.5 %shard_map.305 = (f32[264,1024]{1,0:T(8,128)}, bf16[256,128]{1,0:T(8,128)(2,1)}, f32[8,1024]{1,0:T(8,128)}, f32[8,128]{1,0:T(8,128)}) custom-call(bf16[128,768]{1,0:T(8,128)(2,1)} %get-tuple-element.86.state_ref, bf16[256,768]{1,0:T(8,128)(2,1)} %get-tuple-element.77.scaled_ref, f32[256,768]{1,0:T(8,128)} %get-tuple-element.78.value_ref, ...), custom_call_target="tpu_custom_call" | custom-call | tf_op jit(solution)/shard_map/pallas_call | solution.py:50
  305.8 4.4 all-to-all-start.1
  326.2 28.7 %all_gather.34 = bf16[256,1792]{1,0:T(8,128)(2,1)S(1)} all-gather(bf16[64,1792]{1,0:T(8,128)(2,1)S(1)} %reduce_sum.127), channel_id=1, replica_groups=mesh['pipe'=2,'row'=4,'col'=4] {'col'}, dimensions={0}, use_global_device_ids=true | all-gather | bytes 1146880 | tf_op jit(solution)/shard_map/all_gather | solution.py:393
  357.8 4.4 add_convert_fusion
  362.2 4.4 copy.75
  384.8 5.0 shard_map.307
  399.3 6.7 %collective-permute-done.23.refs_2_ = bf16[144,768]{1,0:T(8,128)(2,1)S(1)} collective-permute-done((bf16[144,768]{1,0:T(8,128)(2,1)S(1)}, bf16[144,768]{1,0:T(8,128)(2,1)S(1)}, u32[]{:S(2)}, u32[]{:S(2)}) %collective-permute-start.23) | collective-permute-done | bytes 221216 | tf_op jit(solution)/shard_map/ppermute | solution.py:369
  406.7 7.4 %shard_map.308 = (f32[264,1024]{1,0:T(8,128)}, bf16[256,128]{1,0:T(8,128)(2,1)}, f32[8,1024]{1,0:T(8,128)}, f32[8,128]{1,0:T(8,128)}) custom-call(bf16[128,768]{1,0:T(8,128)(2,1)} %get-tuple-element.99.state_ref, bf16[256,768]{1,0:T(8,128)(2,1)} %get-tuple-element.68.scaled_ref, f32[256,768]{1,0:T(8,128)} %get-tuple-element.69.value_ref, ...), custom_call_target="tpu_custom_call" | custom-call | tf_op jit(solution)/shard_map/pallas_call | solution.py:50
  429.5 4.3 copy.73
  435.1 25.0 %all_to_all.15 = bf16[4,64,1792]{2,1,0:T(8,128)(2,1)S(1)} all-to-all(bf16[4,64,1792]{2,1,0:T(8,128)(2,1)S(1)} %bitcast.136), channel_id=1, replica_groups=mesh['pipe'=2,'row'=4,'col'=4] {'col'}, dimensions={0} | all-to-all | bytes 1835008 | tf_op jit(solution)/shard_map/all_to_all | solution.py:387
  460.3 19.7 %all_gather.35 = bf16[256,1792]{1,0:T(8,128)(2,1)S(1)} all-gather(bf16[64,1792]{1,0:T(8,128)(2,1)S(1)} %reduce_sum.130), channel_id=1, replica_groups=mesh['pipe'=2,'row'=4,'col'=4] {'col'}, dimensions={0}, use_global_device_ids=true | all-gather | bytes 1146880 | tf_op jit(solution)/shard_map/all_gather | solution.py:393
  507.3 37.9 %psum.23 = f32[2,1280]{1,0:T(2,128)S(1)} all-reduce(f32[2,1280]{1,0:T(2,128)S(1)} %pad_maximum_fusion.25), channel_id=1, replica_groups=mesh['pipe'=2,'row'=4,'col'=4] {'pipe','row','col'}, use_global_device_ids=true, to_apply=%region_19.20 | all-reduce | flops 2560 | bytes 20480 | tf_op jit(solution)/shard_map/psum | solution.py:666
  556.7 29.7 %psum.22 = f32[2,6180]{1,0:T(2,128)S(1)} all-reduce(f32[2,6180]{1,0:T(2,128)S(1)} %pad_maximum_fusion.22), channel_id=1, replica_groups=mesh['pipe'=2,'row'=4,'col'=4] {'pipe','row'}, use_global_device_ids=true, to_apply=%region_14.15 | all-reduce | flops 12360 | bytes 98880 | tf_op jit(solution)/shard_map/psum | solution.py:665
  (492 shorter events, 249.4 us)
Async XLA Ops:
  7.2 42.7 %all-gather.6.cloned.1.call-start = ((), (), s32[]{:S(2)}) async-start(), calls=%async_computation.7 | async-start | bytes 2457600 | tf_op jit(solution)/shard_map/all_gather | solution.py:435
  12.8 76.8 %all-gather.8.cloned.1.call-start = ((), (), s32[]{:S(2)}) async-start(), calls=%async_computation.8 | async-start | bytes 2949120 | tf_op jit(solution)/shard_map/all_gather | solution.py:436
  17.6 111.7 %all-gather.12.cloned.1.call-start = ((), (), s32[]{:S(2)}) async-start(), calls=%async_computation.10 | async-start | bytes 2949120 | tf_op jit(solution)/shard_map/all_gather | solution.py:438
  18.4 160.1 %all-gather.10.cloned.1.call-start = ((), (), s32[]{:S(2)}) async-start(), calls=%async_computation.9 | async-start | bytes 2457600 | tf_op jit(solution)/shard_map/all_gather | solution.py:437
  49.8 79.5 %collective-permute-start.2 = (bf16[1536,640]{1,0:T(8,128)(2,1)}, bf16[1536,640]{1,0:T(8,128)(2,1)}, u32[]{:S(2)}, u32[]{:S(2)}) collective-permute-start(bf16[1536,640]{1,0:T(8,128)(2,1)} %all-gather.6.cloned.1.call-done), channel_id=1, source_target_pairs={{0,16},{16,0},{1,17},{17,1},{2,18},{18,2},{3,19},{19,3},{4,20},{20... | collective-permute-start | bytes 5898248 | tf_op jit(solution)/shard_map/ppermute | solution.py:369
  89.6 64.9 %collective-permute-start.6 = (bf16[1536,768]{0,1:T(8,128)(2,1)}, bf16[1536,768]{0,1:T(8,128)(2,1)}, u32[]{:S(2)}, u32[]{:S(2)}) collective-permute-start(bf16[1536,768]{0,1:T(8,128)(2,1)} %all-gather.8.cloned.1.call-done), channel_id=1, source_target_pairs={{0,16},{16,0},{1,17},{17,1},{2,18},{18,2},{3,19},{19,3},{4,20},{20... | collective-permute-start | bytes 7077896 | tf_op jit(solution)/shard_map/ppermute | solution.py:369
  129.4 51.2 %collective-permute-start.12 = (bf16[1536,768]{0,1:T(8,128)(2,1)}, bf16[1536,768]{0,1:T(8,128)(2,1)}, u32[]{:S(2)}, u32[]{:S(2)}) collective-permute-start(bf16[1536,768]{0,1:T(8,128)(2,1)} %all-gather.12.cloned.1.call-done), channel_id=1, source_target_pairs={{0,16},{16,0},{1,17},{17,1},{2,18},{18,2},{3,19},{19,3},{4,20},{20... | collective-permute-start | bytes 7077896 | tf_op jit(solution)/shard_map/ppermute | solution.py:369
  146.5 15.8 %collective-permute-start.8 = (bf16[144,768]{1,0:T(8,128)(2,1)}, bf16[144,768]{1,0:T(8,128)(2,1)S(1)}, u32[]{:S(2)}, u32[]{:S(2)}) collective-permute-start(bf16[144,768]{1,0:T(8,128)(2,1)} %get-tuple-element.74), channel_id=1, source_target_pairs={{0,8},{4,12},{1,9},{5,13},{2,10},{6,14},{3,11},{7,15},{16,24},{20,... | collective-permute-start | bytes 663560 | tf_op jit(solution)/shard_map/ppermute | solution.py:369
  171.2 26.1 %all-to-all-start = ((bf16[4,64,1664]{2,1,0:T(8,128)(2,1)}), bf16[4,64,1664]{2,1,0:T(8,128)(2,1)S(1)}, u32[]{:S(2)}, u32[]{:S(2)}) async-start(bf16[4,64,1664]{2,1,0:T(8,128)(2,1)} %bitcast.26), calls=%async_computation | async-start | bytes 1703936 | tf_op jit(solution)/shard_map/all_to_all | solution.py:387
  178.4 38.4 %collective-permute-start.10 = (bf16[1536,640]{1,0:T(8,128)(2,1)}, bf16[1536,640]{1,0:T(8,128)(2,1)}, u32[]{:S(2)}, u32[]{:S(2)}) collective-permute-start(bf16[1536,640]{1,0:T(8,128)(2,1)} %all-gather.10.cloned.1.call-done), channel_id=1, source_target_pairs={{0,16},{16,0},{1,17},{17,1},{2,18},{18,2},{3,19},{19,3},{4,20},{20... | collective-permute-start | bytes 5898248 | tf_op jit(solution)/shard_map/ppermute | solution.py:369
  229.0 17.3 %collective-permute-start.13 = (bf16[144,768]{1,0:T(8,128)(2,1)}, bf16[144,768]{1,0:T(8,128)(2,1)S(1)}, u32[]{:S(2)}, u32[]{:S(2)}) collective-permute-start(bf16[144,768]{1,0:T(8,128)(2,1)} %get-tuple-element.83), channel_id=1, source_target_pairs={{0,4},{4,8},{8,12},{1,5},{5,9},{9,13},{2,6},{6,10},{10,14},{3,7},{... | collective-permute-start | bytes 663560 | tf_op jit(solution)/shard_map/ppermute | solution.py:369
  268.9 17.0 %collective-permute-start.17 = (bf16[144,768]{1,0:T(8,128)(2,1)}, bf16[144,768]{1,0:T(8,128)(2,1)S(1)}, u32[]{:S(2)}, u32[]{:S(2)}) collective-permute-start(bf16[144,768]{1,0:T(8,128)(2,1)} %get-tuple-element.95), channel_id=1, source_target_pairs={{4,0},{8,4},{12,8},{5,1},{9,5},{13,9},{6,2},{10,6},{14,10},{7,3},{... | collective-permute-start | bytes 663560 | tf_op jit(solution)/shard_map/ppermute | solution.py:369
  305.8 19.1 %all-to-all-start.1 = ((bf16[4,64,1792]{2,1,0:T(8,128)(2,1)}), bf16[4,64,1792]{2,1,0:T(8,128)(2,1)}, u32[]{:S(2)}, u32[]{:S(2)}) async-start(bf16[4,64,1792]{2,1,0:T(8,128)(2,1)} %bitcast.135), calls=%async_computation.1 | async-start | bytes 1835008 | tf_op jit(solution)/shard_map/all_to_all | solution.py:387
  310.1 176.0 %all-reduce.10.cloned.1.call-start = ((), (), s32[]{:S(2)}) async-start(), calls=%async_computation.11 | async-start | bytes 1572864 | tf_op jit(solution)/shard_map/psum | solution.py:589
  313.1 44.7 %collective-permute-start.27 = (bf16[1536,768]{0,1:T(8,128)(2,1)}, bf16[1536,768]{0,1:T(8,128)(2,1)}, u32[]{:S(2)}, u32[]{:S(2)}) collective-permute-start(bf16[1536,768]{0,1:T(8,128)(2,1)} %pad_maximum_fusion.1), channel_id=1, source_target_pairs={{0,16},{16,0},{1,17},{17,1},{2,18},{18,2},{3,19},{19,3},{4,20},{20... | collective-permute-start | bytes 7077896 | tf_op jit(solution)/shard_map/ppermute | solution.py:369
  316.6 276.3 %reduce-scatter.15.cloned.1.call-start = ((), (), s32[]{:S(2)}) async-start(), calls=%async_computation.15 | async-start | bytes 2949120
  366.6 228.6 %reduce-scatter.13.cloned.1.call-start = ((), (), s32[]{:S(2)}) async-start(), calls=%async_computation.14 | async-start | bytes 2949120
  379.2 46.6 %collective-permute-start.26 = (bf16[1536,768]{0,1:T(8,128)(2,1)}, bf16[1536,768]{0,1:T(8,128)(2,1)}, u32[]{:S(2)}, u32[]{:S(2)}) collective-permute-start(bf16[1536,768]{0,1:T(8,128)(2,1)} %pad_maximum_fusion), channel_id=1, source_target_pairs={{0,16},{16,0},{1,17},{17,1},{2,18},{18,2},{3,19},{19,3},{4,20},{20... | collective-permute-start | bytes 7077896 | tf_op jit(solution)/shard_map/ppermute | solution.py:369
  382.2 17.1 %collective-permute-start.22 = (bf16[144,768]{1,0:T(8,128)(2,1)S(1)}, bf16[144,768]{1,0:T(8,128)(2,1)S(1)}, u32[]{:S(2)}, u32[]{:S(2)}) collective-permute-start(bf16[144,768]{1,0:T(8,128)(2,1)S(1)} %copy-done.84), channel_id=1, source_target_pairs={{8,0},{12,4},{9,1},{13,5},{10,2},{14,6},{11,3},{15,7},{24,16},{28,... | collective-permute-start | bytes 663560 | tf_op jit(solution)/shard_map/ppermute | solution.py:369
  383.5 22.5 %collective-permute-start.23 = (bf16[144,768]{1,0:T(8,128)(2,1)S(1)}, bf16[144,768]{1,0:T(8,128)(2,1)S(1)}, u32[]{:S(2)}, u32[]{:S(2)}) collective-permute-start(bf16[144,768]{1,0:T(8,128)(2,1)S(1)} %copy-done.84), channel_id=1, source_target_pairs={{12,0},{13,1},{14,2},{15,3},{28,16},{29,17},{30,18},{31,19}} | collective-permute-start | bytes 663560 | tf_op jit(solution)/shard_map/ppermute | solution.py:369
  433.8 167.4 %reduce-scatter.9.cloned.1.call-start = ((), (), s32[]{:S(2)}) async-start(), calls=%async_computation.12 | async-start | bytes 2457600 | tf_op jit(solution)/shard_map/reduce_scatter | solution.py:640
  497.0 104.2 %reduce-scatter.11.cloned.1.call-start = ((), (), s32[]{:S(2)}) async-start(), calls=%async_computation.13 | async-start | bytes 2457600 | tf_op jit(solution)/shard_map/reduce_scatter | solution.py:640
  506.5 46.3 %collective-permute-start.30 = (bf16[1536,640]{1,0:T(8,128)(2,1)}, bf16[1536,640]{1,0:T(8,128)(2,1)}, u32[]{:S(2)}, u32[]{:S(2)}) collective-permute-start(bf16[1536,640]{1,0:T(8,128)(2,1)} %convolution_convert_fusion), channel_id=1, source_target_pairs={{0,16},{16,0},{1,17},{17,1},{2,18},{18,2},{3,19},{19,3},{4,20},{20... | collective-permute-start | bytes 5898248 | tf_op jit(solution)/shard_map/ppermute | solution.py:369
  552.7 36.2 %collective-permute-start.25 = (f32[256,1536]{1,0:T(8,128)}, f32[256,1536]{1,0:T(8,128)}, u32[]{:S(2)}, u32[]{:S(2)}) collective-permute-start(f32[256,1536]{1,0:T(8,128)} %fusion.78), channel_id=1, source_target_pairs={{0,16},{16,0},{1,17},{17,1},{2,18},{18,2},{3,19},{19,3},{4,20},{20... | collective-permute-start | bytes 4718600 | tf_op jit(solution)/shard_map/ppermute | solution.py:369
  (106 other events, 1180.1 us)
Sparse Core Ops, SparseCore 0:
  13.0 36.8 all-gather.5
  52.2 37.3 all-gather.7
  92.0 37.3 all-gather.11
  131.6 36.4 all-gather.9
  316.7 56.5 all-reduce.9
  376.2 46.4 reduce-scatter.14
  433.9 35.0 reduce-scatter.12
  497.1 31.8 reduce-scatter.8
  556.7 35.2 reduce-scatter.10

commit v2 on v1

v2 whole, which is shorter than its diff:
```python
import functools
import math

import jax
import jax.numpy as jnp
from jax import lax
from jax.experimental import pallas as pl
from jax.experimental.pallas import tpu as pltpu
from jax.sharding import PartitionSpec as P

EPSILON = 1e-05
LOG2E = math.log2(math.e)
LANE = 128
F32 = jnp.float32
BF16 = jnp.bfloat16
SMALL_ROWS = 16
LEAD = 16
TAPS_ROWS = 32
SMALL = 48
BLOCKS = 4


def dot_nn(a, b):
    return lax.dot_general(a, b, (((1,), (0,)), ((), ())), preferred_element_type=F32)


def dot_nt(a, b):
    return lax.dot_general(a, b, (((1,), (1,)), ((), ())), preferred_element_type=F32)


def dot_tn(a, b):
    return lax.dot_general(a, b, (((0,), (0,)), ((), ())), preferred_element_type=F32)


def dot_exact(a, b):
    return lax.dot_general(
        a, b, (((1,), (0,)), ((), ())), precision=lax.Precision.HIGHEST, preferred_element_type=F32
    )


def sigmoid(v):
    return 1.0 / (1.0 + jnp.exp(-v))


def split_pair(v):
    high = v.astype(BF16)
    return high, (v - high.astype(F32)).astype(BF16)


def on_chip(kernel, out_shapes, scratch=()):
    whole = pl.BlockSpec(memory_space=pltpu.VMEM)
    scalar = pl.BlockSpec(memory_space=pltpu.SMEM)

    def call(*operands):
        return pl.pallas_call(
            kernel,
            out_shape=out_shapes,
            in_specs=[scalar if o.dtype == jnp.int32 else whole for o in operands],
            out_specs=jax.tree.map(lambda _: whole, out_shapes),
            scratch_shapes=scratch,
            compiler_params=pltpu.CompilerParams(vmem_limit_bytes=60 * 1024 * 1024),
        )(*operands)

    return call


def shaped(shape, dtype=F32):
    return jax.ShapeDtypeStruct(shape, dtype)


def tile_of(q):
    return slice(q * LANE, (q + 1) * LANE)


def spread(columns, q, heads_tile, lane_head):
    first = q * heads_tile
    out = columns[:, first : first + 1]
    for i in range(1, heads_tile):
        out = jnp.where(lane_head == i, columns[:, first + i : first + i + 1], out)
    return out


def lane_heads(rows, heads_tile):
    lanes = lax.broadcasted_iota(jnp.int32, (rows, LANE), 1)
    return lanes // (LANE // heads_tile)


def tri_mask(tokens, seg_col, seg_row, transposed):
    first = lax.broadcasted_iota(jnp.int32, (tokens, tokens), 0)
    second = lax.broadcasted_iota(jnp.int32, (tokens, tokens), 1)
    order = first <= second if transposed else first >= second
    return order & (seg_col == seg_row)


def pack_a_kernel(core_ref, value_ref, state_ref, step_ref, keep_ref, give_ref):
    half = value_ref.shape[1] // 2
    heads = step_ref.shape[1]
    core = core_ref[0]
    for ref, place in ((keep_ref, core), (give_ref, 1 - core)):
        ref[:, :half] = value_ref[:, pl.ds(pl.multiple_of(place * half, LANE), half)]
        ref[:, half : half + LANE] = state_ref[:, pl.ds(pl.multiple_of(place * LANE, LANE), LANE)]
        ref[:, half + LANE :] = jnp.zeros((ref.shape[0], LANE), BF16)
        ref[:, half + LANE : half + LANE + heads] = step_ref[...]


def pack_b_kernel(core_ref, gate_ref, out_ref, keep_ref, give_ref):
    half = gate_ref.shape[1] // 2
    core = core_ref[0]
    for ref, place in ((keep_ref, core), (give_ref, 1 - core)):
        ref[:, :half] = gate_ref[:, pl.ds(pl.multiple_of(place * half, LANE), half)]
        ref[:, half:] = out_ref[pl.ds(pl.multiple_of(place * half, LANE), half), :].astype(F32).T.astype(BF16)


def enter_kernel(
    inner, heads_tile, places, core_ref, x_ref, before_ref, small_ref, aux_ref, *refs,
):
    taps_ref, heads_ref, gain_ref, _ = views(small_ref, places)
    mine, other = refs[:BLOCKS], refs[BLOCKS : 2 * BLOCKS]
    (
        normed_ref, scale_ref, z_ref, conv_ref, value_ref, scaled_ref, bc_ref, step_ref, cum_ref, cumt_ref, lead_ref,
        carry_ref, msg_ref, leadu_ref,
    ) = refs[2 * BLOCKS :]
    tokens, width = x_ref.shape
    half = inner // 2
    conv_width = conv_ref.shape[1]
    for ref, at in ((before_ref, slice(0, LEAD)), (x_ref, slice(LEAD, LEAD + tokens))):
        x = ref[...].astype(F32)
        scale = lax.rsqrt(jnp.mean(x * x, axis=1, keepdims=True) + EPSILON)
        normed_ref[at, :] = (x * scale * gain_ref[0:1, :]).astype(BF16)
    scale_ref[...] = jnp.broadcast_to(scale, scale_ref.shape)
    core = core_ref[0]
    block = width // BLOCKS
    for pieces, place in ((mine, core), (other, 1 - core)):
        z = None
        for i in range(BLOCKS):
            term = dot_nn(normed_ref[:, i * block : (i + 1) * block], pieces[i][...])
            z = term if z is None else z + term
        z_ref[:, pl.ds(pl.multiple_of(place * half, LANE), half)] = z[:, :half]
        z_ref[:, pl.ds(pl.multiple_of(inner + place * LANE, LANE), LANE)] = z[:, half : half + LANE]
        if pieces is mine:
            z_ref[:, conv_width:] = z[:, half + LANE :]
    aux = aux_ref[...]
    raw = z_ref[LEAD:, conv_width:] + heads_ref[0:1, :]
    step = jnp.maximum(raw, 0.0) + jnp.log1p(jnp.exp(-jnp.abs(raw)))
    rates = -step * jnp.exp(heads_ref[1:2, :])
    rows = lax.broadcasted_iota(jnp.int32, (tokens, tokens), 0)
    cols = lax.broadcasted_iota(jnp.int32, (tokens, tokens), 1)
    cum = dot_exact((rows >= cols).astype(F32), rates) * LOG2E
    lead = aux[:, 5:6] * jnp.exp2(cum[tokens - 1 : tokens, :] - cum)
    carry = aux[:, 4:5] * jnp.exp2(cum)
    step_ref[...] = step
    cum_ref[...] = cum
    cumt_ref[...] = cum.T
    lead_ref[...] = lead
    carry_ref[...] = carry
    lane_head = lane_heads(tokens, heads_tile)
    for q in range(conv_width // LANE):
        at = tile_of(q)
        acc = taps_ref[4:5, at] + taps_ref[3:4, at] * z_ref[LEAD:, at]
        for j in range(3):
            shifted = z_ref[LEAD - 3 + j : LEAD - 3 + j + tokens, at]
            acc = acc + taps_ref[j : j + 1, at] * (aux[:, j : j + 1] * shifted)
        conv_ref[:, at] = acc
        value = acc * sigmoid(acc)
        if q < inner // LANE:
            value_ref[:, at] = value
            scaled = spread(step, q, heads_tile, lane_head) * value
            scaled_ref[:, at] = scaled.astype(BF16)
            leadu_ref[:, at] = (spread(lead, q, heads_tile, lane_head) * scaled).astype(BF16)
        else:
            bc_ref[:, tile_of(q - inner // LANE)] = value.astype(BF16)
    msg_ref[0:LANE, :] = dot_tn(bc_ref[:, :LANE], leadu_ref[...]).astype(BF16)
    put_through(msg_ref, carry[tokens - 1 : tokens, :], inner, heads_tile)


def enter_first_kernel(
    inner, heads_tile, places, core_ref, x_ref, before_ref, small_ref, seg_ref, seg_before_ref, *refs,
):
    weights, refs = refs[: 2 * BLOCKS], refs[2 * BLOCKS :]
    aux_ref, segt_ref, *made, seg_ext_ref, leadu_ref = refs
    tokens = x_ref.shape[0]
    seg = seg_ref[...]
    seg_ext_ref[0:LEAD, :] = seg_before_ref[...]
    seg_ext_ref[LEAD:, :] = seg
    lanes = lax.broadcasted_iota(jnp.int32, (tokens, LANE), 1)
    flags = jnp.where(lanes == 3, seg, 0.0)
    for j in range(3):
        same = (seg_ext_ref[LEAD - 3 + j : LEAD - 3 + j + tokens, :] == seg).astype(F32)
        flags = jnp.where(lanes == j, same, flags)
    flags = jnp.where(lanes == 4, (seg == seg_ext_ref[LEAD - 1 : LEAD, :]).astype(F32), flags)
    flags = jnp.where(lanes == 5, (seg == seg[tokens - 1 :, :]).astype(F32), flags)
    aux_ref[...] = flags
    segt_ref[...] = seg.T[0:8, :]
    enter_kernel(
        inner, heads_tile, places, core_ref, x_ref, before_ref, small_ref, aux_ref, *weights, *made, leadu_ref
    )


def views(ref, places):
    return tuple(ref.at[:, p] for p in places)


def put_through(msg_ref, last, inner, heads_tile):
    msg_ref[LANE:, :] = jnp.zeros((SMALL_ROWS, inner), BF16)
    lane_row = lane_heads(1, heads_tile)
    for q in range(inner // LANE):
        high, low = split_pair(spread(last, q, heads_tile, lane_row))
        msg_ref[LANE : LANE + 1, tile_of(q)] = high
        msg_ref[LANE + 1 : LANE + 2, tile_of(q)] = low


def wide_kernel(offset, lead, core_ref, a_ref, *refs):
    mine, other = refs[:BLOCKS], refs[BLOCKS : 2 * BLOCKS]
    out_ref = refs[2 * BLOCKS]
    core = core_ref[0]
    half = out_ref.shape[1] // 2
    block = a_ref.shape[1] // BLOCKS
    for pieces, place in ((mine, core), (other, 1 - core)):
        total = None
        for i in range(BLOCKS):
            term = dot_nn(a_ref[lead:, i * block : (i + 1) * block], pieces[i][:, offset : offset + half])
            total = term if total is None else total + term
        out_ref[:, pl.ds(pl.multiple_of(place * half, LANE), half)] = total


def intra_kernel(
    inner, heads_tile, places, scaled_ref, value_ref, bc_ref, cum_ref, cumt_ref, aux_ref, segt_ref, small_ref,
    out_ref,
):
    heads_ref = views(small_ref, places)[1]
    tokens = scaled_ref.shape[0]
    scores = dot_nt(bc_ref[:, LANE:], bc_ref[:, :LANE])
    scores = jnp.where(tri_mask(tokens, aux_ref[:, 3:4], segt_ref[0:1, :], False), scores, 0.0)
    lane_head = lane_heads(tokens, heads_tile)
    lane_row = lane_heads(1, heads_tile)
    for q in range(inner // LANE):
        at = tile_of(q)
        total = spread(heads_ref[2:3, :], q, heads_tile, lane_row) * value_ref[:, at]
        scaled = scaled_ref[:, at]
        for i in range(heads_tile):
            h = q * heads_tile + i
            gap = jnp.minimum(cum_ref[:, h : h + 1] - cumt_ref[h : h + 1, :], 0.0)
            mixed = (jnp.exp2(gap) * scores).astype(BF16)
            total = total + jnp.where(lane_head == i, dot_nn(mixed, scaled), 0.0)
        out_ref[:, at] = total


def enter_states(messages):
    state = None
    for message in reversed(messages):
        own = message[0:LANE, :].astype(F32)
        through = message[LANE : LANE + 1, :].astype(F32) + message[LANE + 1 : LANE + 2, :].astype(F32)
        state = own if state is None else own + through * state
    return state


def gate_kernel(
    inner, heads_tile, places, count, with_grad, core_ref, intra_ref, bc_ref, carry_ref, gate_ref, small_ref, *refs
):
    gain_ref = views(small_ref, places)[3]
    messages = refs[:count]
    mine, other = refs[count : count + BLOCKS], refs[count + BLOCKS : count + 2 * BLOCKS]
    refs = refs[count + 2 * BLOCKS :]
    if with_grad:
        branch_grad_ref, refs = refs[0], refs[1:]
        ssd_ref, state_ref, msg_ref, sums_ref, gated_ref = refs
    else:
        ssd_ref, state_ref, msg_ref, gated_ref = refs
    tokens = intra_ref.shape[0]
    state = enter_states([m[...] for m in messages]).astype(BF16)
    state_ref[...] = state
    inter = dot_nn(bc_ref[:, LANE:], state)
    lane_head = lane_heads(tokens, heads_tile)
    carry = carry_ref[...]
    squares = jnp.zeros((tokens, LANE), F32)
    products = jnp.zeros((tokens, LANE), F32)
    for q in range(inner // LANE):
        at = tile_of(q)
        ssd = intra_ref[:, at] + spread(carry, q, heads_tile, lane_head) * inter[:, at]
        ssd_ref[:, at] = ssd
        gate = gate_ref[:, at]
        gated = ssd * (gate * sigmoid(gate))
        squares = squares + gated * gated
        scaled = gated * gain_ref[0:1, at]
        gated_ref[:, at] = scaled.astype(BF16)
        if with_grad:
            products = products + scaled * branch_grad_ref[:, at]
    half = inner // 2
    core = core_ref[0]
    low = gated_ref[:, pl.ds(pl.multiple_of(core * half, LANE), half)]
    high = gated_ref[:, pl.ds(pl.multiple_of((1 - core) * half, LANE), half)]
    block = mine[0].shape[0]
    for i in range(BLOCKS):
        part = dot_nt(low, mine[i][:, half:]) + dot_nt(high, other[i][:, half:])
        msg_ref[:, i * block : (i + 1) * block] = part.astype(BF16)
    total = jnp.sum(squares, axis=1, keepdims=True)
    lanes = lax.broadcasted_iota(jnp.int32, (tokens, LANE), 1)
    if with_grad:
        packed = jnp.where(lanes == 0, total, 0.0)
        packed = packed + jnp.where(lanes == 1, jnp.sum(products, axis=1, keepdims=True), 0.0)
        sums_ref[...] = packed.T[0:8, :]
    else:
        rest = total - total.astype(BF16).astype(F32)
        packed = jnp.where(lanes == 0, total, jnp.where(lanes == 1, rest, 0.0))
        msg_ref[:, BLOCKS * block :] = packed.astype(BF16)


def ungate_kernel(
    inner, heads_tile, places, norm_width, branch_grad_ref, norm_ref, gate_ref, ssd_ref, small_ref, carry_ref, bc_ref,
    gssd_ref, ggate_ref, branch_ref, msg_ref, ggain_ref, cg_ref,
):
    gain_ref = views(small_ref, places)[3]
    tokens = branch_grad_ref.shape[0]
    rho = norm_ref[:, 0:1]
    pull = norm_ref[:, 1:2] * (rho * rho * rho / norm_width)
    lane_head = lane_heads(tokens, heads_tile)
    carry = carry_ref[...]
    ggain_ref[...] = jnp.zeros(ggain_ref.shape, F32)
    for q in range(inner // LANE):
        at = tile_of(q)
        gate = gate_ref[:, at]
        sig = sigmoid(gate)
        ssd = ssd_ref[:, at]
        gated = ssd * (gate * sig)
        grad = branch_grad_ref[:, at]
        gain = gain_ref[0:1, at]
        normed = gated * rho
        ggain_ref[0:1, at] = jnp.sum(grad * normed, axis=0, keepdims=True)
        branch_ref[:, at] = (normed * gain).astype(BF16)
        ggated = rho * (gain * grad) - gated * pull
        gssd = ggated * (gate * sig)
        gssd_ref[:, at] = gssd
        ggate_ref[:, at] = (ggated * ssd * (sig * (1.0 + gate * (1.0 - sig)))).astype(BF16)
        cg_ref[:, at] = (spread(carry, q, heads_tile, lane_head) * gssd).astype(BF16)
    msg_ref[0:LANE, :] = dot_tn(bc_ref[:, LANE:], cg_ref[...]).astype(BF16)
    put_through(msg_ref, carry[tokens - 1 : tokens, :], inner, heads_tile)


def intra_grad_kernel(
    inner, heads_tile, scaled_ref, gssd_ref, bc_ref, cum_ref, cumt_ref, aux_ref, segt_ref,
    gscaled_ref, gbc_ref, gcum_ref, sums_ref,
):
    tokens = scaled_ref.shape[0]
    mask = tri_mask(tokens, aux_ref[:, 3:4], segt_ref[0:1, :], True)
    scores = jnp.where(mask, dot_nt(bc_ref[:, :LANE], bc_ref[:, LANE:]), 0.0)
    lane_head = lane_heads(tokens, heads_tile)
    gscores = jnp.zeros((tokens, tokens), F32)
    gcum_ref[...] = jnp.zeros(gcum_ref.shape, F32)
    sums_ref[...] = jnp.zeros(sums_ref.shape, F32)
    for q in range(inner // LANE):
        at = tile_of(q)
        grad = gssd_ref[:, at].astype(BF16)
        scaled = scaled_ref[:, at]
        total = jnp.zeros((tokens, LANE), F32)
        for i in range(heads_tile):
            h = q * heads_tile + i
            gap = jnp.minimum(cumt_ref[h : h + 1, :] - cum_ref[:, h : h + 1], 0.0)
            decay = jnp.exp2(gap)
            mixed = decay * scores
            picked = jnp.where(lane_head == i, scaled, jnp.zeros_like(scaled))
            gmixed = dot_nt(picked, grad)
            total = total + jnp.where(lane_head == i, dot_nn(mixed.astype(BF16), grad), 0.0)
            product = gmixed * mixed
            sums_ref[h : h + 1, :] = jnp.sum(product, axis=0, keepdims=True)
            gcum_ref[:, h : h + 1] = -jnp.sum(product, axis=1, keepdims=True)
            gscores = gscores + gmixed * decay
        gscaled_ref[:, at] = total
    gscores = jnp.where(mask, gscores, 0.0)
    gbc_ref[:, :LANE] = dot_nn(gscores.astype(BF16), bc_ref[:, LANE:])
    gbc_ref[:, LANE:] = dot_nn(gscores.T.astype(BF16), bc_ref[:, :LANE])
    gcum_ref[...] = gcum_ref[...] + sums_ref[...].T


def inter_grad_kernel(
    inner, heads_tile, places, count, state_ref, scaled_ref, value_ref, gssd_ref, gscaled_ref, bc_ref, gbc_ref, gcum_ref,
    step_ref, lead_ref, carry_ref, z_ref, conv_ref, aux_ref, small_ref, ggain_ref, *refs,
):
    taps_ref, heads_ref, _, _ = views(small_ref, places)
    messages = refs[:count]
    gpre_ref, gstep_ref, gtaps_ref, em_ref, leadu_ref, cg_ref, gain_ref, lose_ref, gsize_ref = refs[count:]
    tokens = scaled_ref.shape[0]
    width = conv_ref.shape[1]
    aux = aux_ref[...]
    adjoint = enter_states([m[...] for m in messages])
    adjoint_low = adjoint.astype(BF16)
    state = state_ref[...]
    from_adjoint = dot_nn(bc_ref[:, :LANE], adjoint_low)
    from_state = dot_nn(bc_ref[:, LANE:], state)
    overlap = jnp.sum(adjoint * state.astype(F32), axis=0, keepdims=True)
    lane_head = lane_heads(tokens, heads_tile)
    lane_row = lane_heads(1, heads_tile)
    step = step_ref[...]
    lead = lead_ref[...]
    carry = carry_ref[...]
    em_ref[0:8, :] = jnp.zeros((8, LANE), F32)
    em_ref[8 + tokens :, :] = jnp.zeros((8, LANE), F32)
    gpre_ref[0:8, :] = jnp.zeros((8, width), F32)
    gtaps_ref[...] = jnp.zeros(gtaps_ref.shape, F32)

    def through_conv(q, grad):
        at = tile_of(q)
        conv = conv_ref[:, at]
        sig = sigmoid(conv)
        e = grad * (sig * (1.0 + conv * (1.0 - sig)))
        gtaps_ref[4:5, at] = jnp.sum(e, axis=0, keepdims=True)
        gtaps_ref[3:4, at] = jnp.sum(e * z_ref[LEAD:, at], axis=0, keepdims=True)
        total = None
        for j in range(3):
            masked = aux[:, j : j + 1] * e
            shifted = z_ref[LEAD - 3 + j : LEAD - 3 + j + tokens, at]
            gtaps_ref[j : j + 1, at] = jnp.sum(masked * shifted, axis=0, keepdims=True)
            em_ref[8 : 8 + tokens, :] = masked
            term = taps_ref[j : j + 1, at] * em_ref[3 - j : 11 - j + tokens, :]
            total = term if total is None else total + term
        gpre_ref[8:LEAD, at] = total[0:8, :]
        gpre_ref[LEAD:, at] = total[8:, :] + taps_ref[3:4, at] * e

    for q in range(inner // LANE):
        at = tile_of(q)
        scaled = scaled_ref[:, at].astype(F32)
        grad = gssd_ref[:, at]
        value = value_ref[:, at]
        leads = spread(lead, q, heads_tile, lane_head)
        carries = spread(carry, q, heads_tile, lane_head)
        pushed = leads * from_adjoint[:, at]
        gscaled = gscaled_ref[:, at] + pushed
        carried = carries * grad
        leadu_ref[:, at] = (leads * scaled).astype(BF16)
        cg_ref[:, at] = carried.astype(BF16)
        gain_ref[:, at] = (carried * from_state[:, at]).astype(BF16)
        lose_ref[:, at] = (scaled * pushed).astype(BF16)
        gsize_ref[:, at] = (gscaled * value).astype(BF16)
        gtaps_ref[5:6, at] = jnp.sum(grad * value, axis=0, keepdims=True)
        gvalue = spread(step, q, heads_tile, lane_head) * gscaled
        gvalue = gvalue + spread(heads_ref[2:3, :], q, heads_tile, lane_row) * grad
        through_conv(q, gvalue)
    gb = gbc_ref[:, :LANE] + dot_nt(leadu_ref[...], adjoint_low)
    gc = gbc_ref[:, LANE:] + dot_nt(cg_ref[...], state)
    through_conv(inner // LANE, gb)
    through_conv(inner // LANE + 1, gc)
    head_of = lax.broadcasted_iota(jnp.int32, (inner, LANE), 0) // (LANE // heads_tile)
    pick = (head_of == lax.broadcasted_iota(jnp.int32, (inner, LANE), 1)).astype(BF16)
    lose = dot_nn(lose_ref[...], pick)
    gcum = gcum_ref[...] + dot_nn(gain_ref[...], pick) - lose
    high, low = split_pair(overlap)
    ends = dot_nn(jnp.broadcast_to(high, (8, inner)), pick) + dot_nn(jnp.broadcast_to(low, (8, inner)), pick)
    last = carry[tokens - 1 : tokens, :] * ends[0:1, :] + jnp.sum(lose, axis=0, keepdims=True)
    row_of = lax.broadcasted_iota(jnp.int32, (tokens, LANE), 0)
    gcum = gcum + jnp.where(row_of == tokens - 1, last, 0.0)
    rows = lax.broadcasted_iota(jnp.int32, (tokens, tokens), 0)
    cols = lax.broadcasted_iota(jnp.int32, (tokens, tokens), 1)
    grate = dot_exact((rows <= cols).astype(F32), gcum)
    speed = jnp.exp(heads_ref[1:2, :])
    gsize = dot_nn(gsize_ref[...], pick) - speed * grate
    raw = z_ref[LEAD:, width:] + heads_ref[0:1, :]
    graw = gsize * sigmoid(raw)
    gstep_ref[...] = graw.astype(BF16)
    gtaps_ref[6:7, :inner] = ggain_ref[0:1, :]
    gtaps_ref[7:8, 0:LANE] = jnp.sum(graw, axis=0, keepdims=True)
    gtaps_ref[7:8, LANE : 2 * LANE] = jnp.sum(grate * (-speed * step), axis=0, keepdims=True)


def give_b_kernel(
    core_ref, ggate_ref, normed_ref, g_out_ref, branch_ref,
    other_b_ref, gg_mine_ref, gg_other_ref, normed_t_ref, g_out_t_ref,
):
    width = g_out_ref.shape[1]
    half = ggate_ref.shape[1] // 2
    core = core_ref[0]
    gg_mine_ref[...] = ggate_ref[:, pl.ds(pl.multiple_of(core * half, LANE), half)]
    gg_other_ref[...] = ggate_ref[:, pl.ds(pl.multiple_of((1 - core) * half, LANE), half)]
    block = width // BLOCKS
    for i in range(BLOCKS):
        at = slice(i * block, (i + 1) * block)
        normed_t_ref[at, :] = normed_ref[LEAD:, at].astype(F32).T.astype(BF16)
        g_out_t_ref[at, :] = g_out_ref[:, at].astype(F32).T.astype(BF16)
    other_b_ref[:, :half] = dot_nn(normed_t_ref[...], gg_other_ref[...]).astype(BF16)
    branch = branch_ref[:, pl.ds(pl.multiple_of((1 - core) * half, LANE), half)]
    other_b_ref[:, half:] = dot_nn(g_out_t_ref[...], branch).astype(BF16)


def keep_b_kernel(core_ref, normed_t_ref, g_out_t_ref, branch_ref, gg_mine_ref, their_ref, *refs):
    size = normed_t_ref.shape[0] // len(refs)
    half = gg_mine_ref.shape[1]
    branch = branch_ref[:, pl.ds(pl.multiple_of(core_ref[0] * half, LANE), half)]
    for i, ref in enumerate(refs):
        at = slice(i * size, (i + 1) * size)
        part = dot_nn(normed_t_ref[at, :], gg_mine_ref[...]) + their_ref[at, :half].astype(F32)
        ref[:, :half] = part.astype(BF16)
        part = dot_nn(g_out_t_ref[at, :], branch) + their_ref[at, half:].astype(F32)
        ref[:, half:] = part.astype(BF16)


def taps_rows(taps, wide):
    left, right = taps[:, :wide], taps[:, wide:]
    right = jnp.concatenate([right, jnp.zeros((8, 2 * wide - taps.shape[1]), F32)], axis=1)
    rows = []
    for part in (left, right):
        high = part.astype(BF16).astype(F32)
        rows += [high, part - high]
    return jnp.concatenate(rows, axis=0).astype(BF16)


def gain_rows(gain, wide):
    high = gain.astype(BF16).astype(F32)
    index = lax.broadcasted_iota(jnp.int32, (16, wide), 0)
    out = jnp.zeros((16, wide), F32)
    count = -(-gain.shape[1] // wide)
    for i in range(count):
        for base, part in ((0, high), (8, gain - high)):
            piece = part[:, i * wide : (i + 1) * wide]
            if piece.shape[1] < wide:
                piece = jnp.concatenate([piece, jnp.zeros((1, wide - piece.shape[1]), F32)], axis=1)
            out = jnp.where(index == base + i, piece, out)
    return out.astype(BF16)


def give_a_kernel(
    core_ref, gpre_ref, next_ref, gstep_ref, normed_t_ref, gtaps_ref, other_a_ref, ga_mine_ref, ga_other_ref, glow_ref
):
    tokens, width = glow_ref.shape
    inner = width - 2 * LANE
    half = inner // 2
    core = core_ref[0]
    cut = tokens - LEAD
    glow_ref[:cut, :] = gpre_ref[LEAD : LEAD + cut, :].astype(BF16)
    glow_ref[cut:, :] = (gpre_ref[LEAD + cut :, :] + next_ref[...]).astype(BF16)
    for ga_ref, place in ((ga_mine_ref, core), (ga_other_ref, 1 - core)):
        ga_ref[:, :half] = glow_ref[:, pl.ds(pl.multiple_of(place * half, LANE), half)]
        ga_ref[:, half : half + LANE] = glow_ref[:, pl.ds(pl.multiple_of(inner + place * LANE, LANE), LANE)]
        ga_ref[:, half + LANE :] = gstep_ref[...]
    rows = normed_t_ref.shape[0]
    other_a_ref[:rows, :] = dot_nn(normed_t_ref[...], ga_other_ref[...]).astype(BF16)
    other_a_ref[rows:, :] = taps_rows(gtaps_ref[...], other_a_ref.shape[1])


def keep_a_kernel(normed_t_ref, ga_mine_ref, their_ref, gtaps_ref, ggain_ref, *refs):
    rows = normed_t_ref.shape[0]
    size = rows // len(refs)
    wide = ga_mine_ref.shape[1]
    theirs = [their_ref[rows + 16 * i : rows + 16 * (i + 1), :].astype(F32) for i in range(2)]
    taps = jnp.concatenate([t[0:8] + t[8:16] for t in theirs], axis=1)[:, : gtaps_ref.shape[1]] + gtaps_ref[...]
    small = taps_rows(taps, wide)
    gain = gain_rows(ggain_ref[0:1, :], wide)
    for i, ref in enumerate(refs):
        at = slice(i * size, (i + 1) * size)
        ref[:size, :] = (dot_nn(normed_t_ref[at, :], ga_mine_ref[...]) + their_ref[at, :].astype(F32)).astype(BF16)
        ref[size : size + TAPS_ROWS, :] = small
        ref[size + TAPS_ROWS :, :] = gain


def pull_kernel(ga_mine_ref, ga_other_ref, gg_mine_ref, gg_other_ref, x_ref, scale_ref, *refs):
    mine_a, other_a, mine_b, other_b = (refs[i * BLOCKS : (i + 1) * BLOCKS] for i in range(4))
    msg_ref, ggain_ref = refs[4 * BLOCKS :]
    half = gg_mine_ref.shape[1]
    block = mine_a[0].shape[0]
    scale = scale_ref[:, 0:1]
    ggain_ref[...] = jnp.zeros(ggain_ref.shape, F32)
    for i in range(BLOCKS):
        at = slice(i * block, (i + 1) * block)
        part = dot_nt(ga_mine_ref[...], mine_a[i][...])
        part = part + dot_nt(ga_other_ref[:, : half + LANE], other_a[i][:, : half + LANE])
        part = part + dot_nt(gg_mine_ref[...], mine_b[i][:, :half])
        part = part + dot_nt(gg_other_ref[...], other_b[i][:, :half])
        msg_ref[:, at] = part.astype(BF16)
        ggain_ref[0:1, at] = jnp.sum(part * (x_ref[:, at].astype(F32) * scale), axis=0, keepdims=True)


def leave_kernel(norm_width, places, below, ordered, row_ref, full_ref, x_ref, scale_ref, small_ref, g_out_ref, *refs):
    gain_ref = views(small_ref, places)[2]
    if below:
        raw_ref, grad_ref, low_ref, norm_ref = refs
    else:
        (grad_ref,) = refs
    tokens, width = x_ref.shape
    scale = scale_ref[:, 0:1]
    x = x_ref[...].astype(F32)
    pulled = full_ref[...].astype(F32) * gain_ref[0:1, :]
    slope = jnp.sum(pulled * x, axis=1, keepdims=True) * (scale * scale * scale / width)
    grad = g_out_ref[...].astype(F32) + scale * pulled - x * slope
    if ordered:
        block = width // BLOCKS
        for i in range(BLOCKS):
            start = pl.multiple_of((row_ref[0] ^ i) * block, LANE)
            grad_ref[:, pl.ds(start, block)] = grad[:, i * block : (i + 1) * block]
    else:
        grad_ref[...] = grad
    if below:
        low = grad.astype(BF16)
        low_ref[...] = low
        dots = jnp.sum(low.astype(F32) * raw_ref[:, :width].astype(F32), axis=1, keepdims=True)
        squares = raw_ref[:, width : width + 1].astype(F32) + raw_ref[:, width + 1 : width + 2].astype(F32)
        lanes = lax.broadcasted_iota(jnp.int32, (tokens, LANE), 1)
        norm_ref[...] = jnp.where(lanes == 0, lax.rsqrt(squares / norm_width + EPSILON), dots)


def permute(block, axis, route):
    return lax.ppermute(block, axis, route)


def from_before(block, count, distance):
    return permute(block, "row", [(i, i + distance) for i in range(count - distance)])


def from_after(block, count, distance):
    return permute(block, "row", [(i + distance, i) for i in range(count - distance)])


def swapped(block):
    return permute(block, "pipe", [(0, 1), (1, 0)])


def exchanged(blocks, axis):
    return lax.all_to_all(blocks, axis, 0, 0)


def spread_out(block, axis):
    count = lax.axis_size(axis)
    return exchanged(jnp.broadcast_to(block[None], (count,) + block.shape), axis).reshape(
        (count * block.shape[0],) + block.shape[1:]
    )


def parts_sum(block, axis):
    count = lax.axis_size(axis)
    parts = exchanged(block.reshape((count, block.shape[0] // count) + block.shape[1:]), axis)
    return jnp.sum(parts.astype(F32), axis=0)


def direct_sum(block, axis):
    parts = [block] + [sent_to(block, axis, b) for b in range(1, lax.axis_size(axis))]
    parts = [p.astype(F32) for p in parts]
    while len(parts) > 1:
        parts = [parts[i] + parts[i + 1] for i in range(0, len(parts), 2)]
    return parts[0]


def sent_to(block, axis, flip):
    count = lax.axis_size(axis)
    return permute(block, axis, [(i, i ^ flip) for i in range(count)])


def relative_order(block, dim, axis, place=None):
    count = lax.axis_size(axis)
    size = block.shape[dim] // count
    place = lax.axis_index(axis) if place is None else place
    return jnp.concatenate(
        [lax.dynamic_slice_in_dim(block, (place ^ b) * size, size, dim) for b in range(count)], axis=dim
    )


class Phases:
    def __init__(self, token):
        self.token = token

    def hold(self, value):
        return lax.optimization_barrier((value, self.token))[0]

    def close(self, *values):
        self.token = lax.optimization_barrier((self.token,) + tuple(jax.tree.leaves(values)))[0]


def after(block, *others):
    return lax.optimization_barrier((block,) + others)[0]


def local(
    inputs, cotangent, segment_ids, batch_order, norm_gain, gate_proj, value_proj, step_proj, state_proj,
    conv_value, conv_value_bias, conv_state, conv_state_bias, step_bias, decay_log, skip_gain, gate_gain, out_proj,
):
    core = lax.axis_index("pipe")
    first = core == 0
    core_id = core.reshape(1).astype(jnp.int32)
    rows = lax.axis_size("row")
    row = lax.axis_index("row")
    tokens, width = inputs.shape[1], inputs.shape[2]
    inner = gate_proj.shape[2]
    heads = step_proj.shape[2]
    states = state_proj.shape[2] // 2
    heads_tile = LANE // (inner // heads)
    half = inner // 2
    conv_width = inner + 2 * states
    norm_width = inner * lax.axis_size("col")
    reach = max(rows // 2, 1)
    distances = range(1, reach + 1)
    group = rows // BLOCKS

    def pick_mine(a, b):
        return jnp.where(first, a, b)

    phases = Phases(core_id)
    hold, close = phases.hold, phases.close

    shard = gate_proj.shape[1]
    a_width, b_width = half + states + LANE, inner
    own_a, away_a = on_chip(pack_a_kernel, (shaped((shard, a_width), BF16),) * 2)(
        core_id, value_proj[0], state_proj[0], step_proj[0]
    )
    close(away_a)
    take_a = swapped(hold(away_a))
    own_b, away_b = on_chip(pack_b_kernel, (shaped((shard, b_width), BF16),) * 2)(core_id, hold(gate_proj[0]), out_proj[0])
    close(take_a, away_b)

    def blocks_of(pieces):
        return [jnp.concatenate(pieces[i * group : (i + 1) * group], axis=0) for i in range(BLOCKS)]

    def both_cores(mine):
        return mine, [swapped(p) for p in mine]

    piece_a0 = hold(pick_mine(own_a, take_a))
    pieces_a0 = [piece_a0] + [sent_to(piece_a0, "row", b) for b in range(1, rows)]
    take_b = swapped(hold(away_b))
    piece_b0 = pick_mine(own_b, take_b)

    taps_own = jnp.concatenate(
        [
            jnp.concatenate([hold(conv_value[0]), conv_state[0]], axis=1),
            jnp.concatenate([conv_value_bias, conv_state_bias], axis=1),
            jnp.zeros((3, conv_width), F32),
        ],
        axis=0,
    )
    heads_own = jnp.pad(jnp.concatenate([hold(step_bias), decay_log, skip_gain], axis=0), ((0, 5), (0, LANE - heads)))
    gains_own = jnp.concatenate([relative_order(hold(norm_gain), 1, "row"), gate_gain], axis=1)
    gains_own = jnp.pad(gains_own, ((0, 7), (0, 0)))
    small = jnp.concatenate([taps_own, heads_own, gains_own], axis=1)
    small_other = swapped(small)
    params = (pick_mine(small, small_other), pick_mine(small_other, small))
    places = (slice(0, conv_width), slice(conv_width, conv_width + LANE))
    places += (slice(conv_width + LANE, conv_width + LANE + width), slice(conv_width + LANE + width, small.shape[1]))

    source = hold(batch_order)[core]
    layer_in = relative_order(inputs[source], 1, "row")
    seg = jnp.broadcast_to(segment_ids[source].astype(F32)[:, None], (tokens, LANE))
    sent_rows = jnp.concatenate([layer_in[tokens - LEAD :], seg[tokens - LEAD :].astype(BF16)], axis=1)
    got_rows = from_before(sent_rows, rows, 1)
    other_order = row ^ jnp.maximum(row - 1, 0)
    before0 = relative_order(got_rows[:, :width], 1, "row", other_order)
    seg_before = jnp.where(row == 0, -1.0, got_rows[:, width:].astype(F32))
    g_out1 = relative_order(hold(cotangent)[core], 1, "row")
    close(pieces_a0, piece_b0, params, layer_in, seg, before0, seg_before, g_out1)

    long = tokens + LEAD
    message_shape = shaped((states + SMALL_ROWS, inner), BF16)
    entered = (
        shaped((long, width), BF16), shaped((tokens, LANE)), shaped((long, conv_width + LANE)),
        shaped((tokens, conv_width)), shaped((tokens, inner)), shaped((tokens, inner), BF16),
        shaped((tokens, 2 * states), BF16), shaped((tokens, LANE)), shaped((tokens, LANE)), shaped((LANE, tokens)),
        shaped((tokens, LANE)), shaped((tokens, LANE)), message_shape,
    )
    enter = [
        on_chip(
            functools.partial(enter_first_kernel, inner, heads_tile, places),
            (shaped((tokens, LANE)), shaped((8, tokens))) + entered,
            [pltpu.VMEM((long, LANE), F32), pltpu.VMEM((tokens, inner), BF16)],
        ),
        on_chip(
            functools.partial(enter_kernel, inner, heads_tile, places), entered, [pltpu.VMEM((tokens, inner), BF16)]
        ),
    ]
    intra = on_chip(functools.partial(intra_kernel, inner, heads_tile, places), shaped((tokens, inner)))
    gate_product = on_chip(functools.partial(wide_kernel, 0, LEAD), shaped((tokens, inner)))
    branch_product = on_chip(functools.partial(wide_kernel, half, 0), shaped((tokens, inner)))
    gates = [
        on_chip(
            functools.partial(gate_kernel, inner, heads_tile, places, reach, with_grad),
            (shaped((tokens, inner)), shaped((states, inner), BF16))
            + ((shaped((tokens, width), BF16), shaped((8, tokens))) if with_grad else (shaped((tokens, width + LANE), BF16),)),
            [pltpu.VMEM((tokens, inner), BF16)],
        )
        for with_grad in (False, True)
    ]
    ungate = on_chip(
        functools.partial(ungate_kernel, inner, heads_tile, places, norm_width),
        (
            shaped((tokens, inner)), shaped((tokens, inner), BF16), shaped((tokens, inner), BF16), message_shape,
            shaped((8, inner)),
        ),
        [pltpu.VMEM((tokens, inner), BF16)],
    )
    intra_grad = on_chip(
        functools.partial(intra_grad_kernel, inner, heads_tile),
        (shaped((tokens, inner)), shaped((tokens, 2 * states)), shaped((tokens, LANE))),
        [pltpu.VMEM((LANE, tokens), F32)],
    )
    inter_grad = on_chip(
        functools.partial(inter_grad_kernel, inner, heads_tile, places, reach),
        (shaped((long, conv_width)), shaped((tokens, LANE), BF16), shaped((8, conv_width))),
        [pltpu.VMEM((tokens + 16, LANE), F32)] + [pltpu.VMEM((tokens, inner), BF16)] * 5,
    )
    pull = on_chip(pull_kernel, (shaped((tokens, width), BF16), shaped((8, width))))
    weight_t = shaped((width, tokens), BF16)
    give_a = on_chip(
        give_a_kernel,
        (shaped((width + TAPS_ROWS, a_width), BF16),) + (shaped((tokens, a_width), BF16),) * 2,
        [pltpu.VMEM((tokens, conv_width), BF16)],
    )
    give_b = on_chip(
        give_b_kernel,
        (shaped((width, b_width), BF16), shaped((tokens, half), BF16), shaped((tokens, half), BF16), weight_t, weight_t),
    )
    keep_a = on_chip(keep_a_kernel, (shaped((shard + SMALL, a_width), BF16),) * rows)
    keep_b = on_chip(keep_b_kernel, (shaped((shard, b_width), BF16),) * rows)
    row_id = row.reshape(1).astype(jnp.int32)
    ordered = rows == BLOCKS and shard % LANE == 0
    leave = [
        on_chip(functools.partial(leave_kernel, norm_width, places, False, ordered), shaped((tokens, width))),
        on_chip(
            functools.partial(leave_kernel, norm_width, places, True, ordered),
            (shaped((tokens, width)), shaped((tokens, width), BF16), shaped((tokens, LANE))),
        ),
    ]

    def in_order(grad):
        return grad if ordered else relative_order(grad, 1, "row")

    weights_a0 = both_cores(blocks_of(pieces_a0))
    held_b0 = hold(piece_b0)
    pieces_b0 = [held_b0] + [sent_to(held_b0, "row", b) for b in range(1, rows - 1)]
    aux, seg_t, *made0 = enter[0](
        core_id, hold(layer_in), before0, params[0], seg, seg_before, *weights_a0[0], *weights_a0[1]
    )
    normed0, scale0, z0, conv0, value0, scaled0, bc0, step0, cum0, cumt0, lead0, carry0, message0 = made0
    close(message0, pieces_b0)
    messages0 = [from_before(hold(message0), rows, d) for d in distances]
    pieces_b0.append(sent_to(hold(held_b0), "row", rows - 1))
    inside0 = intra(hold(scaled0), value0, bc0, cum0, cumt0, aux, seg_t, params[0])
    close(messages0, inside0, pieces_b0)
    weights_b0 = both_cores(blocks_of(pieces_b0))
    gate0 = gate_product(core_id, hold(normed0), *weights_b0[0], *weights_b0[1])
    ssd0, state0, partial0 = gates[0](
        core_id, inside0, bc0, carry0, gate0, params[0], *messages0, *weights_b0[0], *weights_b0[1]
    )
    close(partial0)
    piece_a1 = hold(pick_mine(take_a, own_a))
    pieces_a1 = [piece_a1] + [sent_to(piece_a1, "row", b) for b in range(1, rows)]
    own0 = parts_sum(hold(partial0), "col")
    square = own0[:, width : width + 1] + own0[:, width + 1 : width + 2]
    rest = square - square.astype(BF16).astype(F32)
    lanes = lax.broadcasted_iota(jnp.int32, own0.shape, 1)
    own0 = jnp.where(lanes == width, square, jnp.where(lanes == width + 1, rest, own0)).astype(BF16)
    close(own0, pieces_a1)
    piece_b1 = hold(pick_mine(take_b, own_b))
    pieces_b1 = [piece_b1] + [sent_to(piece_b1, "row", b) for b in range(1, rows)]
    weights_a1 = both_cores([hold(w) for w in blocks_of(pieces_a1)])
    full0 = spread_out(hold(own0), "col")
    close(full0, weights_a1, pieces_b1)
    full0 = hold(full0)
    squares0 = full0[:, width : width + 1].astype(F32) + full0[:, width + 1 : width + 2].astype(F32)
    rho0 = lax.rsqrt(squares0 / norm_width + EPSILON)
    x1 = (layer_in.astype(F32) + rho0 * full0[:, :width].astype(F32)).astype(BF16)

    before1 = relative_order(from_before(x1[tokens - LEAD :], rows, 1), 1, "row", other_order)
    close(x1, before1)
    weights_b1 = both_cores([hold(w) for w in blocks_of(pieces_b1)])
    made1 = enter[1](core_id, hold(x1), before1, params[1], aux, *weights_a1[0], *weights_a1[1])
    normed1, scale1, z1, conv1, value1, scaled1, bc1, step1, cum1, cumt1, lead1, carry1, message1 = made1
    close(message1, weights_b1)
    messages1 = [from_before(hold(message1), rows, d) for d in distances]
    inside1 = intra(hold(scaled1), value1, bc1, cum1, cumt1, aux, seg_t, params[1])
    gate1 = gate_product(core_id, hold(normed1), *weights_b1[0], *weights_b1[1])
    close(messages1, inside1, gate1)
    gbranch1 = branch_product(core_id, hold(g_out1), *weights_b1[0], *weights_b1[1])
    ssd1, state1, partial1, sums1 = gates[1](
        core_id, inside1, bc1, carry1, gate1, params[1], *messages1, *weights_b1[0], *weights_b1[1], gbranch1
    )
    totals1 = direct_sum(sums1, "col")
    close(totals1)
    rho1 = lax.rsqrt(totals1[0] / norm_width + EPSILON)[:, None]
    norm1 = jnp.pad(jnp.concatenate([rho1, totals1[1][:, None]], axis=1), ((0, 0), (0, LANE - 2)))

    def scan_back(layer, gbranch, norm, gate, ssd, state, made, beside):
        _, scale, z, conv, value, scaled, bc, step, cum, cumt, lead, carry, _ = made
        gssd, ggate, branch, message, ggain = ungate(gbranch, norm, gate, ssd, params[layer], carry, bc)
        close(message)
        messages = [from_after(hold(message), rows, d) for d in distances]
        gscaled, gbc, gcum = intra_grad(scaled, hold(gssd), bc, cum, cumt, aux, seg_t)
        close(messages, gscaled, beside("intra"))
        gpre, gstep, gtaps = inter_grad(
            state, scaled, value, gssd, hold(gscaled), bc, gbc, gcum, step, lead, carry, z, conv, aux, params[layer],
            ggain, *messages,
        )
        close(gpre)
        return gpre, gstep, gtaps, ggate, branch

    def reduce_back(scanned, normed, scale, x, g_out, weights_a, weights_b, beside):
        gpre, gstep, gtaps, ggate, branch = scanned
        from_next = from_after(hold(gpre[:LEAD]), rows, 1)
        other_b, gg_mine, gg_other, normed_t, g_out_t = give_b(core_id, hold(ggate), normed, g_out, branch)
        close(from_next, other_b, beside("halo"))
        their_b = swapped(hold(other_b))
        other_a, ga_mine, ga_other = give_a(core_id, gpre, hold(from_next), gstep, normed_t, gtaps)
        close(their_b, other_a, beside("give"))
        their_a = swapped(hold(other_a))
        partial, ggain = pull(
            hold(ga_mine), ga_other, gg_mine, gg_other, x, scale,
            *weights_a[0], *weights_a[1], *weights_b[0], *weights_b[1],
        )
        close(their_a, partial, beside("pull"))
        ggain = hold(ggain)
        ggain = relative_order(ggain + swapped(ggain), 1, "row")
        kept_b = keep_b(core_id, hold(normed_t), g_out_t, branch, gg_mine, their_b)
        kept_a = keep_a(normed_t, ga_mine, their_a, gtaps, ggain)
        close(kept_a, kept_b, beside("keep"))
        got_a = [sent_to(hold(v), "row", b) for b, v in enumerate(kept_a) if b]
        own = parts_sum(hold(partial), "col").astype(BF16)
        close(own, got_a, beside("scatter"))
        share_a = functools.reduce(lambda u, v: u + v.astype(F32), got_a, hold(kept_a[0]).astype(F32))
        got_b = [sent_to(hold(v), "row", b) for b, v in enumerate(kept_b) if b]
        full = spread_out(hold(own), "col")
        close(full, got_b, beside("gather", share_a))
        share_b = functools.reduce(lambda u, v: u + v.astype(F32), got_b, hold(kept_b[0]).astype(F32))
        return hold(full), share_a, share_b

    places_of = lax.broadcasted_iota(jnp.int32, (2, 1, 1), 0)

    def both_batches(below, above, place):
        mine, theirs = pick_mine(below, above), swapped(pick_mine(above, below))
        return jnp.where(places_of == place, mine[None], theirs[None])

    def settled(own, others):
        mine = pick_mine(own, others).astype(BF16)
        theirs = swapped(pick_mine(others, own).astype(BF16))
        return pick_mine(mine, theirs).astype(F32), pick_mine(theirs, mine).astype(F32)

    def state_part(share):
        return share[:shard, half : half + states].astype(BF16)

    cols = lax.axis_size("col")
    col = lax.axis_index("col")
    chunk = tokens // cols
    slots = ("intra", "halo", "pull")
    parts1 = [lax.dynamic_slice_in_dim(hold(partial1), (col ^ b) * chunk, chunk, 0) for b in range(cols)]
    received = {1: [], 0: []}
    store = {}

    def exchange(layer, name, sources):
        if name not in slots:
            return ()
        at = slots.index(name)
        mine = range(1 + at, cols) if name == slots[-1] else range(1 + at, min(2 + at, cols))
        got = [sent_to(hold(sources[b]), "col", b) for b in mine]
        received[layer] += got
        return got

    def beside1(name, share=None):
        return exchange(1, name, parts1)

    def beside0(name, share=None):
        got = list(exchange(0, name, [store["chunk"]] * cols))
        if name == "give":
            store["state"] = hold(store["state"])
            store["state_got"] = sent_to(store["state"], "col", 1)
            got.append(store["state_got"])
        if name == "keep":
            total = store["state"].astype(F32) + hold(store["state_got"]).astype(F32)
            reach_out = 2
            while reach_out < cols:
                total = total.astype(BF16)
                total = total.astype(F32) + sent_to(total, "col", reach_out).astype(F32)
                reach_out *= 2
            store["state"] = total
            got.append(total)
        if name == "scatter":
            raw1 = relative_order(jnp.concatenate([store["chunk"]] + received[0], axis=0), 0, "col")
            x2 = (hold(x1).astype(F32) + rho1 * raw1.astype(F32)).astype(BF16)
            store["outputs"] = both_batches(relative_order(x1, 1, "row"), relative_order(x2, 1, "row"), core)
            got.append(store["outputs"])
        if name == "gather":
            store["a"] = settled(share[:shard], share_a1[:shard])
            got.append(store["a"])
        return got

    scanned1 = scan_back(1, gbranch1, norm1, gate1, ssd1, state1, made1, beside1)
    grad_full1, share_a1, share_b1 = reduce_back(
        scanned1, normed1, scale1, x1, g_out1, weights_a1, weights_b1, beside1
    )
    store["chunk"] = functools.reduce(lambda u, v: u + v.astype(F32), received[1], parts1[0].astype(F32)).astype(BF16)
    store["state"] = state_part(share_a1)
    g_in1, g_out0, norm0 = leave[1](row_id, grad_full1, x1, scale1, params[1], g_out1, full0)
    gbranch0 = branch_product(core_id, g_out0, *weights_b0[0], *weights_b0[1])
    scanned0 = scan_back(0, gbranch0, norm0, gate0, ssd0, state0, made0, beside0)
    grad_full0, share_a0, share_b0 = reduce_back(
        scanned0, normed0, scale0, layer_in, g_out0, weights_a0, weights_b0, beside0
    )
    g_in0 = leave[0](row_id, grad_full0, layer_in, scale0, params[0], g_out0)
    close(g_in0)
    layer_outputs = store["outputs"]
    input_grads = both_batches(in_order(hold(g_in0)), in_order(g_in1), jnp.where(first, batch_order[0], core))

    small_sums = pick_mine(share_a0[shard:], share_a1[shard:])
    vec = jnp.concatenate([small_sums[0:8] + small_sums[8:16], small_sums[16:24] + small_sums[24:32]], axis=1)
    vec = vec[:, :conv_width]
    gain_sum = small_sums[TAPS_ROWS : TAPS_ROWS + 8] + small_sums[TAPS_ROWS + 8 :]
    partial_sums = jnp.concatenate([vec[:, inner:], gain_sum], axis=1)
    tiles = partial_sums.shape[1] // LANE
    high, low = split_pair(partial_sums)
    both = jnp.concatenate([high, low], axis=0)
    message = jnp.concatenate([hold(state_part(share_a0))] + [both[:, tile_of(i)] for i in range(tiles)], axis=0)
    summed = direct_sum(message, "col")
    state_sum0, rest_sum = summed[:shard], summed[shard:].reshape(tiles, 16, LANE)
    rest_sum = rest_sum[:, 0:8] + rest_sum[:, 8:16]
    vec_state = jnp.concatenate([rest_sum[i] for i in range(2)], axis=1)
    ggain_in = jnp.concatenate([rest_sum[i] for i in range(2, tiles)], axis=1)
    ggain_in = ggain_in[: -(-width // a_width)].reshape(1, -1)[:, :width]
    d_skip = vec[5, :inner].reshape(heads, inner // heads).sum(axis=1)

    a_low, a_high = store["a"]
    s_low, s_high = settled(state_sum0, store["state"])
    b_low, b_high = settled(share_b0, share_b1)
    d_value = jnp.concatenate([a_low[:, :half], a_high[:, :half]], axis=1)
    d_state = jnp.concatenate([s_low, s_high], axis=1)
    d_step = a_low[:, half + states : half + states + heads]
    d_gate = jnp.concatenate([b_low[:, :half], b_high[:, :half]], axis=1)
    d_out = jnp.concatenate([b_low[:, half:], b_high[:, half:]], axis=1).T

    return (
        layer_outputs[None],
        input_grads[None],
        ggain_in,
        d_gate[None],
        d_value[None],
        d_step[None],
        d_state[None],
        vec[None, 0:4, :inner],
        vec[4:5, :inner],
        vec_state[None, 0:4],
        vec_state[4:5],
        vec[7:8, :heads],
        vec[7:8, LANE : LANE + heads],
        d_skip[None],
        vec[6:7, :inner],
        d_out[None],
    )


def solution(mesh):
    in_specs = (
        P(None, "row", None),
        P(None, "row", None),
        P(None, "row"),
        P(),
        P("pipe", None),
        P("pipe", "row", "col"),
        P("pipe", "row", "col"),
        P("pipe", "row", "col"),
        P("pipe", "row", None),
        P("pipe", None, "col"),
        P("pipe", "col"),
        P("pipe", None, None),
        P("pipe", None),
        P("pipe", "col"),
        P("pipe", "col"),
        P("pipe", "col"),
        P("pipe", "col"),
        P("pipe", "col", "row"),
    )
    out_specs = (
        P("pipe", None, "row", None),
        P("pipe", None, "row", None),
        P("pipe", None),
        P("pipe", "row", "col"),
        P("pipe", "row", "col"),
        P("pipe", "row", "col"),
        P("pipe", "row", None),
        P("pipe", None, "col"),
        P("pipe", "col"),
        P("pipe", None, None),
        P("pipe", None),
        P("pipe", "col"),
        P("pipe", "col"),
        P("pipe", "col"),
        P("pipe", "col"),
        P("pipe", "col", "row"),
    )
    return jax.shard_map(local, mesh=mesh, in_specs=in_specs, out_specs=out_specs, check_vma=False)
```

time: 628 us -> 543 us (0.86)
  blocking collectives: 173 us -> 0 us
  Pallas kernels: 54.2 us -> 145 us
  matrix products: 73.9 us -> 0 us
  starting transfers between devices: 51.5 us -> 124 us
  waiting for transfers between devices: 136 us -> 190 us
  local copies, waits for them, and re-layouts: 49.3 us -> 26.8 us
  other arithmetic: 61.1 us -> 40.8 us
  between operations: 18.7 us -> 4.57 us
    ppermute x32 -> x80, waiting for transfers between devices: 24.3 us -> 148 us  [permute(): return lax.ppermute(block, axis, route)]
    all_gather x4 -> x0, waiting for transfers between devices: 93.3 us -> none  [the longest x1 39 us: local(): mine_b = [gather(pick_mine(keep_b, take_b))]]
    pallas_call x12 -> x30, Pallas kernels: 54.2 us -> 145 us  [call(): pl.pallas_call(kernel, out_shape=out_shapes, in_specs=[scalar if o.dtype...]
    all_gather x4 -> x0, blocking collectives: 80.1 us -> none  [the longest x3 66.8 us: col_gather(): return lax.all_gather(block, 'col', axis=0, tiled=True)]
    dot_general x36 -> x0, matrix products: 73.9 us -> none  [the longest x12 27.4 us: dot_tn(): lax.dot_general(a, b, (((0,), (0,)), ((), ())), preferred_element_type=F32)]
    psum x2 -> x0, blocking collectives: 67.7 us -> none  [the longest x1 37.9 us: local(): part_sum = lax.psum(jnp.stack([part0, part1]), ('pipe', 'row', 'col'))]
    ppermute x32 -> x80, starting transfers between devices: 42.2 us -> 95.7 us  [permute(): return lax.ppermute(block, axis, route)]
    all_to_all x2 -> x6, waiting for transfers between devices: 17.5 us -> 42.7 us  [exchanged(): return lax.all_to_all(blocks, axis, 0, 0)]
  transfers between devices with their start and end apart: 43 -> 86, of which waited for: 14 -> 38; matrix products, arithmetic and copies ran while one was open for 26% -> 8% of each run, Pallas kernels for 6% -> 16%
where the time goes in v2:
time: 543 us; the launch traced here: 532 us
  waiting for transfers between devices  190 us (35%)
  Pallas kernels  145 us (27%)
  starting transfers between devices  124 us (23%)
  other arithmetic  40.8 us (8%)
  local copies, waits for them, and re-layouts  26.8 us (5%)
    ppermute x80, waiting for transfers between devices, permute(): return lax.ppermute(block, axis, route)  148 us
    pallas_call x30, Pallas kernels, call(): pl.pallas_call(kernel, out_shape=out_shapes, in_specs=[scalar if o.dtype...  145 us
    ppermute x80, starting transfers between devices, permute(): return lax.ppermute(block, axis, route)  95.7 us
    all_to_all x6, waiting for transfers between devices, exchanged(): return lax.all_to_all(blocks, axis, 0, 0)  42.7 us
    all_to_all x6, starting transfers between devices, exchanged(): return lax.all_to_all(blocks, axis, 0, 0)  28.6 us
    unnamed x186, local copies, waits for them, and re-layouts  12.4 us
  transfers between devices with their start and end apart: 86, of which 38 were waited for; matrix products, arithmetic and copies ran while one was open for 8% of the time, Pallas kernels for 16%

profile of v2, /device:TPU:0, one launch (start us, length us, event | category | flops | bytes accessed | tf_op | source)
XLA Modules:
  0.0 532.2 jit_solution(7298971250617902175)
XLA Ops:
  22.8 12.7 %collective-permute-done.6 = bf16[16,1664]{1,0:T(8,128)(2,1)S(1)} collective-permute-done((bf16[16,1664]{1,0:T(8,128)(2,1)S(1)}, bf16[16,1664]{1,0:T(8,128)(2,1)S(1)}, u32[]{:S(2)}, u32[]{:S(2)}) %collective-permute-start.6) | collective-permute-done | bytes 53280 | tf_op jit(solution)/shard_map/ppermute | solution.py:598
  49.0 8.2 %shard_map.299 = (f32[256,128]{1,0:T(8,128)}, f32[8,256]{1,0:T(8,128)}, bf16[272,1536]{1,0:T(8,128)(2,1)}, f32[256,128]{1,0:T(8,128)}, f32[272,1152]{1,0:T(8,128...) custom-call(s32[1]{0:T(128)} %bitcast.core_ref, ...), custom_call_target="tpu_custom_call" | custom-call | tf_op jit(solution)/shard_map/pallas_call | solution.py:55
  60.3 13.6 %collective-permute-done.15.refs_3_.refs_5_.refs_11_ = bf16[384,768]{1,0:T(8,128)(2,1)S(1)} collective-permute-done((bf16[384,768]{1,0:T(8,128)(2,1)S(1)}, bf16[384,768]{1,0:T(8,128)(2,1)S(1)}, u32[]{:S(2)}, u32[]{:S(2)}) %collective-permute-start.15) | collective-permute-done | bytes 589856 | tf_op jit(solution)/shard_map/ppermute | solution.py:598
  82.1 6.8 %collective-permute-start.14 = (bf16[144,768]{1,0:T(8,128)(2,1)}, bf16[144,768]{1,0:T(8,128)(2,1)}, u32[]{:S(2)}, u32[]{:S(2)}) collective-permute-start(bf16[144,768]{1,0:T(8,128)(2,1)} %get-tuple-element.266), channel_id=1, source_target_pairs={{0,8},{4,12},{1,9},{5,13},{2,10},{6,14},{3,11},{7,15},{16,24},{20,... | collective-permute-start | bytes 663560 | tf_op jit(solution)/shard_map/ppermute | solution.py:598
  98.4 5.6 %shard_map.302 = (f32[256,768]{1,0:T(8,128)}, bf16[128,768]{1,0:T(8,128)(2,1)}, bf16[256,1664]{1,0:T(8,128)(2,1)}) custom-call(s32[1]{0:T(128)} %bitcast.core_ref, f32[256,768]{1,0:T(8,128)} %shard_map.300.intra_ref, bf16[256,256]{1,0:T(8,128)(2,1)} %get-tuple-element.259.bc_ref, f32[256,128]{1,0:T(8,128)} %get-tuple-element.264.carry_ref, ...), custom_call_target="tpu_custom_call" | custom-call | tf_op jit(solution)/shard_map/pallas_call | solution.py:55
  113.0 16.5 %all-to-all-done = bf16[4,64,1664]{2,1,0:T(8,128)(2,1)S(1)} async-done(((bf16[4,64,1664]{2,1,0:T(8,128)(2,1)}), bf16[4,64,1664]{2,1,0:T(8,128)(2,1)S(1)}, u32[]{:S(2)}, u32[]{:S(2)}) %all-to-all-start) | async-done | bytes 852000 | tf_op jit(solution)/shard_map/all_to_all | solution.py:614
  146.1 9.9 %collective-permute-done.27.refs_1_.refs_3_.refs_9_ = bf16[384,768]{1,0:T(8,128)(2,1)S(1)} collective-permute-done((bf16[384,768]{1,0:T(8,128)(2,1)S(1)}, bf16[384,768]{1,0:T(8,128)(2,1)S(1)}, u32[]{:S(2)}, u32[]{:S(2)}) %collective-permute-start.27) | collective-permute-done | bytes 589856 | tf_op jit(solution)/shard_map/ppermute | solution.py:598
  156.0 12.0 %collective-permute-done.28.refs_2_.refs_4_.refs_10_ = bf16[384,768]{1,0:T(8,128)(2,1)S(1)} collective-permute-done((bf16[384,768]{1,0:T(8,128)(2,1)S(1)}, bf16[384,768]{1,0:T(8,128)(2,1)S(1)}, u32[]{:S(2)}, u32[]{:S(2)}) %collective-permute-start.28) | collective-permute-done | bytes 589856 | tf_op jit(solution)/shard_map/ppermute | solution.py:598
  177.6 7.8 %shard_map.303 = (bf16[272,1536]{1,0:T(8,128)(2,1)}, f32[256,128]{1,0:T(8,128)}, f32[272,1152]{1,0:T(8,128)}, f32[256,1024]{1,0:T(8,128)}, f32[256,768]{1,0:T(8,...) custom-call(s32[1]{0:T(128)} %bitcast.core_ref, ...), custom_call_target="tpu_custom_call" | custom-call | tf_op jit(solution)/shard_map/pallas_call | solution.py:55
  206.5 6.0 %shard_map.307 = (f32[256,768]{1,0:T(8,128)}, bf16[128,768]{1,0:T(8,128)(2,1)}, bf16[256,1536]{1,0:T(8,128)(2,1)}, f32[8,256]{1,0:T(8,128)}) custom-call(s32[1]{0:T(128)} %bitcast.core_ref, f32[256,768]{1,0:T(8,128)} %shard_map.304.intra_ref, bf16[256,256]{1,0:T(8,128)(2,1)} %get-tuple-element.295.bc_ref, f32[256,128]{1,0:T(8,128)} %get-tuple-element.301.carry_ref, ...), custom_call_target="tpu_custom_call" | custom-call | tf_op jit(solution)/shard_map/pallas_call | solution.py:55
  237.1 7.4 %shard_map.310 = (f32[272,1024]{1,0:T(8,128)}, bf16[256,128]{1,0:T(8,128)(2,1)}, f32[8,1024]{1,0:T(8,128)}) custom-call(bf16[128,768]{1,0:T(8,128)(2,1)} %get-tuple-element.316.state_ref, bf16[256,768]{1,0:T(8,128)(2,1)} %get-tuple-element.293.scaled_ref, f32[256,768]{1,0:T(8,128)} %get-tuple-element.294.value_ref, f32[256,768]{1,0:T(8,128)} %get-tuple-element.310.gssd_ref, ...), custom_call_target="tpu_custom_call" | custom-call | tf_op jit(solution)/shard_map/pallas_call | solution.py:55
  262.0 7.5 %shard_map.313 = (bf16[256,1536]{1,0:T(8,128)(2,1)}, f32[8,1536]{1,0:T(8,128)}) custom-call(bf16[256,640]{1,0:T(8,128)(2,1)} %get-tuple-element.343.ga_mine_ref, bf16[256,640]{1,0:T(8,128)(2,1)} %get-tuple-element.344.ga_other_ref, bf16[256,384]{1,0:T(8,128)(2,1)} %get-tuple-element.345.gg_mine_ref, bf16[256,384]{1,0:T(8,128)(2,1)} %get-tuple-element.346.gg_other_ref, ...), custom_call_target="tpu_custom_call" | custom-call | tf_op jit(solution)/shard_map/pallas_call | solution.py:55
  278.9 5.6 %all-to-all-start.2 = ((bf16[4,64,1536]{2,1,0:T(8,128)(2,1)}), bf16[4,64,1536]{2,1,0:T(8,128)(2,1)S(1)}, u32[]{:S(2)}, u32[]{:S(2)}) async-start(bf16[4,64,1536]{2,1,0:T(8,128)(2,1)} %bitcast.23), calls=%async_computation.2 | async-start | bytes 1572864 | tf_op jit(solution)/shard_map/all_to_all | solution.py:614
  290.3 15.0 %all-to-all-done.2 = bf16[4,64,1536]{2,1,0:T(8,128)(2,1)S(1)} async-done(((bf16[4,64,1536]{2,1,0:T(8,128)(2,1)}), bf16[4,64,1536]{2,1,0:T(8,128)(2,1)S(1)}, u32[]{:S(2)}, u32[]{:S(2)}) %all-to-all-start.2) | async-done | bytes 786464 | tf_op jit(solution)/shard_map/all_to_all | solution.py:614
  305.4 10.0 %collective-permute-done.50 = bf16[432,640]{1,0:T(8,128)(2,1)S(1)} collective-permute-done((bf16[432,640]{1,0:T(8,128)(2,1)}, bf16[432,640]{1,0:T(8,128)(2,1)S(1)}, u32[]{:S(2)}, u32[]{:S(2)}) %collective-permute-start.50) | collective-permute-done | bytes 552992 | tf_op jit(solution)/shard_map/ppermute | solution.py:598
  324.7 13.0 %collective-permute-done.52 = bf16[384,768]{1,0:T(8,128)(2,1)S(1)} collective-permute-done((bf16[384,768]{1,0:T(8,128)(2,1)}, bf16[384,768]{1,0:T(8,128)(2,1)S(1)}, u32[]{:S(2)}, u32[]{:S(2)}) %collective-permute-start.52) | collective-permute-done | bytes 589856 | tf_op jit(solution)/shard_map/ppermute | solution.py:598
  337.7 10.7 %collective-permute-done.53 = bf16[384,768]{1,0:T(8,128)(2,1)S(1)} collective-permute-done((bf16[384,768]{1,0:T(8,128)(2,1)}, bf16[384,768]{1,0:T(8,128)(2,1)S(1)}, u32[]{:S(2)}, u32[]{:S(2)}) %collective-permute-start.53) | collective-permute-done | bytes 589856 | tf_op jit(solution)/shard_map/ppermute | solution.py:598
  373.5 7.4 %shard_map.320 = (f32[272,1024]{1,0:T(8,128)}, bf16[256,128]{1,0:T(8,128)(2,1)}, f32[8,1024]{1,0:T(8,128)}) custom-call(bf16[128,768]{1,0:T(8,128)(2,1)} %get-tuple-element.386.state_ref, bf16[256,768]{1,0:T(8,128)(2,1)} %get-tuple-element.257.scaled_ref, f32[256,768]{1,0:T(8,128)} %get-tuple-element.258.value_ref, f32[256,768]{1,0:T(8,128)} %get-tuple-element.382.gssd_ref, ...), custom_call_target="tpu_custom_call" | custom-call | tf_op jit(solution)/shard_map/pallas_call | solution.py:55
  400.6 7.5 %shard_map.323 = (bf16[256,1536]{1,0:T(8,128)(2,1)}, f32[8,1536]{1,0:T(8,128)}) custom-call(bf16[256,640]{1,0:T(8,128)(2,1)} %get-tuple-element.415.ga_mine_ref, bf16[256,640]{1,0:T(8,128)(2,1)} %get-tuple-element.416.ga_other_ref, bf16[256,384]{1,0:T(8,128)(2,1)} %get-tuple-element.417.gg_mine_ref, bf16[256,384]{1,0:T(8,128)(2,1)} %get-tuple-element.418.gg_other_ref, ...), custom_call_target="tpu_custom_call" | custom-call | tf_op jit(solution)/shard_map/pallas_call | solution.py:55
  430.7 5.2 collective-permute-start.67
  439.9 11.2 %all-to-all-done.4 = bf16[4,64,1536]{2,1,0:T(8,128)(2,1)S(1)} async-done(((bf16[4,64,1536]{2,1,0:T(8,128)(2,1)}), bf16[4,64,1536]{2,1,0:T(8,128)(2,1)S(1)}, u32[]{:S(2)}, u32[]{:S(2)}) %all-to-all-start.4) | async-done | bytes 786464 | tf_op jit(solution)/shard_map/all_to_all | solution.py:614
  451.3 10.3 %collective-permute-done.68 = bf16[432,640]{1,0:T(8,128)(2,1)} collective-permute-done((bf16[432,640]{1,0:T(8,128)(2,1)}, bf16[432,640]{1,0:T(8,128)(2,1)}, u32[]{:S(2)}, u32[]{:S(2)}) %collective-permute-start.68) | collective-permute-done | bytes 552992 | tf_op jit(solution)/shard_map/ppermute | solution.py:598
  479.9 7.7 %collective-permute-done.70 = bf16[384,768]{1,0:T(8,128)(2,1)} collective-permute-done((bf16[384,768]{1,0:T(8,128)(2,1)}, bf16[384,768]{1,0:T(8,128)(2,1)}, u32[]{:S(2)}, u32[]{:S(2)}) %collective-permute-start.70) | collective-permute-done | bytes 589856 | tf_op jit(solution)/shard_map/ppermute | solution.py:598
  487.6 12.3 %collective-permute-done.71 = bf16[384,768]{1,0:T(8,128)(2,1)} collective-permute-done((bf16[384,768]{1,0:T(8,128)(2,1)}, bf16[384,768]{1,0:T(8,128)(2,1)}, u32[]{:S(2)}, u32[]{:S(2)}) %collective-permute-start.71) | collective-permute-done | bytes 589856 | tf_op jit(solution)/shard_map/ppermute | solution.py:598
  (473 shorter events, 297.9 us)
Async XLA Ops:
  10.1 28.9 %collective-permute-start.1 = (bf16[384,640]{1,0:T(8,128)(2,1)S(1)}, bf16[384,640]{1,0:T(8,128)(2,1)}, u32[]{:S(2)}, u32[]{:S(2)}) collective-permute-start(bf16[384,640]{1,0:T(8,128)(2,1)S(1)} %get-tuple-element.244.refs_0_), channel_id=1, source_target_pairs={{0,4},{4,0},{8,12},{12,8},{1,5},{5,1},{9,13},{13,9},{2,6},{6,2},{1... | collective-permute-start | bytes 1474568 | tf_op jit(solution)/shard_map/ppermute | solution.py:598
  12.7 26.4 %collective-permute-start.2 = (bf16[384,640]{1,0:T(8,128)(2,1)S(1)}, bf16[384,640]{1,0:T(8,128)(2,1)}, u32[]{:S(2)}, u32[]{:S(2)}) collective-permute-start(bf16[384,640]{1,0:T(8,128)(2,1)S(1)} %get-tuple-element.244.refs_0_), channel_id=1, source_target_pairs={{0,8},{4,12},{8,0},{12,4},{1,9},{5,13},{9,1},{13,5},{2,10},{6,14},... | collective-permute-start | bytes 1474568 | tf_op jit(solution)/shard_map/ppermute | solution.py:598
  14.2 24.8 %collective-permute-start.3 = (bf16[384,640]{1,0:T(8,128)(2,1)S(1)}, bf16[384,640]{1,0:T(8,128)(2,1)S(1)}, u32[]{:S(2)}, u32[]{:S(2)}) collective-permute-start(bf16[384,640]{1,0:T(8,128)(2,1)S(1)} %get-tuple-element.244.refs_0_), channel_id=1, source_target_pairs={{0,12},{4,8},{8,4},{12,0},{1,13},{5,9},{9,5},{13,1},{2,14},{6,10},... | collective-permute-start | bytes 1474568 | tf_op jit(solution)/shard_map/ppermute | solution.py:598
  14.2 31.0 %collective-permute-start.7 = (bf16[384,640]{1,0:T(8,128)(2,1)S(1)}, bf16[384,640]{1,0:T(8,128)(2,1)}, u32[]{:S(2)}, u32[]{:S(2)}) collective-permute-start(bf16[384,640]{1,0:T(8,128)(2,1)S(1)} %get-tuple-element.244.refs_0_), channel_id=1, source_target_pairs={{0,16},{16,0},{1,17},{17,1},{2,18},{18,2},{3,19},{19,3},{4,20},{20... | collective-permute-start | bytes 1474568 | tf_op jit(solution)/shard_map/ppermute | solution.py:598
  59.7 33.3 %collective-permute-start.16 = (bf16[384,768]{1,0:T(8,128)(2,1)S(1)}, bf16[384,768]{1,0:T(8,128)(2,1)S(1)}, u32[]{:S(2)}, u32[]{:S(2)}) collective-permute-start(bf16[384,768]{1,0:T(8,128)(2,1)S(1)} %get-tuple-element.267.refs_0_.refs_2_.refs_8_), channel_id=1, source_target_pairs={{0,16},{16,0},{1,17},{17,1},{2,18},{18,2},{3,19},{19,3},{4,20},{20... | collective-permute-start | bytes 1769480 | tf_op jit(solution)/shard_map/ppermute | solution.py:598
  59.7 33.3 %collective-permute-start.17 = (bf16[384,768]{1,0:T(8,128)(2,1)S(1)}, bf16[384,768]{1,0:T(8,128)(2,1)}, u32[]{:S(2)}, u32[]{:S(2)}) collective-permute-start(bf16[384,768]{1,0:T(8,128)(2,1)S(1)} %collective-permute-done.11.refs_1_.refs_3_.refs_9_), channel_id=1, source_target_pairs={{0,16},{16,0},{1,17},{17,1},{2,18},{18,2},{3,19},{19,3},{4,20},{20... | collective-permute-start | bytes 1769480 | tf_op jit(solution)/shard_map/ppermute | solution.py:598
  60.3 32.8 %collective-permute-start.18 = (bf16[384,768]{1,0:T(8,128)(2,1)S(1)}, bf16[384,768]{1,0:T(8,128)(2,1)}, u32[]{:S(2)}, u32[]{:S(2)}) collective-permute-start(bf16[384,768]{1,0:T(8,128)(2,1)S(1)} %collective-permute-done.12.refs_2_.refs_4_.refs_10_), channel_id=1, source_target_pairs={{0,16},{16,0},{1,17},{17,1},{2,18},{18,2},{3,19},{19,3},{4,20},{20... | collective-permute-start | bytes 1769480 | tf_op jit(solution)/shard_map/ppermute | solution.py:598
  104.0 25.5 %all-to-all-start = ((bf16[4,64,1664]{2,1,0:T(8,128)(2,1)}), bf16[4,64,1664]{2,1,0:T(8,128)(2,1)S(1)}, u32[]{:S(2)}, u32[]{:S(2)}) async-start(bf16[4,64,1664]{2,1,0:T(8,128)(2,1)} %bitcast.92), calls=%async_computation | async-start | bytes 1703936 | tf_op jit(solution)/shard_map/all_to_all | solution.py:614
  134.3 33.8 %all-to-all-start.1 = ((bf16[4,64,1664]{2,1,0:T(8,128)(2,1)}), bf16[4,64,1664]{2,1,0:T(8,128)(2,1)}, u32[]{:S(2)}, u32[]{:S(2)}) async-start(bf16[4,64,1664]{2,1,0:T(8,128)(2,1)} %broadcast_in_dim.141), calls=%async_computation.1 | async-start | bytes 1703936 | tf_op jit(solution)/shard_map/all_to_all | solution.py:614
  140.4 27.6 %collective-permute-start.28 = (bf16[384,768]{1,0:T(8,128)(2,1)S(1)}, bf16[384,768]{1,0:T(8,128)(2,1)S(1)}, u32[]{:S(2)}, u32[]{:S(2)}) collective-permute-start(bf16[384,768]{1,0:T(8,128)(2,1)S(1)} %get-tuple-element.286.refs_0_.refs_2_.refs_8_), channel_id=1, source_target_pairs={{0,8},{4,12},{8,0},{12,4},{1,9},{5,13},{9,1},{13,5},{2,10},{6,14},... | collective-permute-start | bytes 1769480 | tf_op jit(solution)/shard_map/ppermute | solution.py:598
  142.1 25.9 %collective-permute-start.29 = (bf16[384,768]{1,0:T(8,128)(2,1)S(1)}, bf16[384,768]{1,0:T(8,128)(2,1)S(1)}, u32[]{:S(2)}, u32[]{:S(2)}) collective-permute-start(bf16[384,768]{1,0:T(8,128)(2,1)S(1)} %get-tuple-element.286.refs_0_.refs_2_.refs_8_), channel_id=1, source_target_pairs={{0,12},{4,8},{8,4},{12,0},{1,13},{5,9},{9,5},{13,1},{2,14},{6,10},... | collective-permute-start | bytes 1769480 | tf_op jit(solution)/shard_map/ppermute | solution.py:598
  278.9 26.4 %all-to-all-start.2 = ((bf16[4,64,1536]{2,1,0:T(8,128)(2,1)}), bf16[4,64,1536]{2,1,0:T(8,128)(2,1)S(1)}, u32[]{:S(2)}, u32[]{:S(2)}) async-start(bf16[4,64,1536]{2,1,0:T(8,128)(2,1)} %bitcast.23), calls=%async_computation.2 | async-start | bytes 1572864 | tf_op jit(solution)/shard_map/all_to_all | solution.py:614
  288.7 26.7 %collective-permute-start.50 = (bf16[432,640]{1,0:T(8,128)(2,1)}, bf16[432,640]{1,0:T(8,128)(2,1)S(1)}, u32[]{:S(2)}, u32[]{:S(2)}) collective-permute-start(bf16[432,640]{1,0:T(8,128)(2,1)} %get-tuple-element.366), channel_id=1, source_target_pairs={{0,8},{4,12},{8,0},{12,4},{1,9},{5,13},{9,1},{13,5},{2,10},{6,14},... | collective-permute-start | bytes 1658888 | tf_op jit(solution)/shard_map/ppermute | solution.py:598
  288.7 26.7 %collective-permute-start.51 = (bf16[432,640]{1,0:T(8,128)(2,1)}, bf16[432,640]{1,0:T(8,128)(2,1)S(1)}, u32[]{:S(2)}, u32[]{:S(2)}) collective-permute-start(bf16[432,640]{1,0:T(8,128)(2,1)} %get-tuple-element.367), channel_id=1, source_target_pairs={{0,12},{4,8},{8,4},{12,0},{1,13},{5,9},{9,5},{13,1},{2,14},{6,10},... | collective-permute-start | bytes 1658888 | tf_op jit(solution)/shard_map/ppermute | solution.py:598
  316.5 31.9 %all-to-all-start.3 = ((bf16[4,64,1536]{2,1,0:T(8,128)(2,1)}), bf16[4,64,1536]{2,1,0:T(8,128)(2,1)S(1)}, u32[]{:S(2)}, u32[]{:S(2)}) async-start(bf16[4,64,1536]{2,1,0:T(8,128)(2,1)} %broadcast_in_dim.142), calls=%async_computation.3 | async-start | bytes 1572864 | tf_op jit(solution)/shard_map/all_to_all | solution.py:614
  321.5 26.9 %collective-permute-start.53 = (bf16[384,768]{1,0:T(8,128)(2,1)}, bf16[384,768]{1,0:T(8,128)(2,1)S(1)}, u32[]{:S(2)}, u32[]{:S(2)}) collective-permute-start(bf16[384,768]{1,0:T(8,128)(2,1)} %get-tuple-element.371), channel_id=1, source_target_pairs={{0,8},{4,12},{8,0},{12,4},{1,9},{5,13},{9,1},{13,5},{2,10},{6,14},... | collective-permute-start | bytes 1769480 | tf_op jit(solution)/shard_map/ppermute | solution.py:598
  322.9 25.4 %collective-permute-start.54 = (bf16[384,768]{1,0:T(8,128)(2,1)}, bf16[384,768]{1,0:T(8,128)(2,1)S(1)}, u32[]{:S(2)}, u32[]{:S(2)}) collective-permute-start(bf16[384,768]{1,0:T(8,128)(2,1)} %get-tuple-element.372), channel_id=1, source_target_pairs={{0,12},{4,8},{8,4},{12,0},{1,13},{5,9},{9,5},{13,1},{2,14},{6,10},... | collective-permute-start | bytes 1769480 | tf_op jit(solution)/shard_map/ppermute | solution.py:598
  423.2 27.9 %all-to-all-start.4 = ((bf16[4,64,1536]{2,1,0:T(8,128)(2,1)}), bf16[4,64,1536]{2,1,0:T(8,128)(2,1)S(1)}, u32[]{:S(2)}, u32[]{:S(2)}) async-start(bf16[4,64,1536]{2,1,0:T(8,128)(2,1)} %bitcast.93), calls=%async_computation.4 | async-start | bytes 1572864 | tf_op jit(solution)/shard_map/all_to_all | solution.py:614
  427.7 91.3 %collective-permute-start.65 = (bf16[384,128]{1,0:T(8,128)(2,1)S(1)}, bf16[384,128]{1,0:T(8,128)(2,1)S(1)}, u32[]{:S(2)}, u32[]{:S(2)}) collective-permute-start(bf16[384,128]{1,0:T(8,128)(2,1)S(1)} %add_convert_fusion.3), channel_id=1, source_target_pairs={{0,2},{1,3},{2,0},{3,1},{4,6},{5,7},{6,4},{7,5},{8,10},{9,11},{10,... | collective-permute-start | bytes 294920 | tf_op jit(solution)/shard_map/ppermute | solution.py:598
  435.9 25.6 %collective-permute-start.68 = (bf16[432,640]{1,0:T(8,128)(2,1)}, bf16[432,640]{1,0:T(8,128)(2,1)}, u32[]{:S(2)}, u32[]{:S(2)}) collective-permute-start(bf16[432,640]{1,0:T(8,128)(2,1)} %get-tuple-element.440), channel_id=1, source_target_pairs={{0,8},{4,12},{8,0},{12,4},{1,9},{5,13},{9,1},{13,5},{2,10},{6,14},... | collective-permute-start | bytes 1658888 | tf_op jit(solution)/shard_map/ppermute | solution.py:598
  435.9 25.6 %collective-permute-start.69 = (bf16[432,640]{1,0:T(8,128)(2,1)}, bf16[432,640]{1,0:T(8,128)(2,1)}, u32[]{:S(2)}, u32[]{:S(2)}) collective-permute-start(bf16[432,640]{1,0:T(8,128)(2,1)} %get-tuple-element.441), channel_id=1, source_target_pairs={{0,12},{4,8},{8,4},{12,0},{1,13},{5,9},{9,5},{13,1},{2,14},{6,10},... | collective-permute-start | bytes 1658888 | tf_op jit(solution)/shard_map/ppermute | solution.py:598
  467.2 32.8 %all-to-all-start.5 = ((bf16[4,64,1536]{2,1,0:T(8,128)(2,1)}), bf16[4,64,1536]{2,1,0:T(8,128)(2,1)S(1)}, u32[]{:S(2)}, u32[]{:S(2)}) async-start(bf16[4,64,1536]{2,1,0:T(8,128)(2,1)} %broadcast_in_dim.146), calls=%async_computation.5 | async-start | bytes 1572864 | tf_op jit(solution)/shard_map/all_to_all | solution.py:614
  471.5 28.5 %collective-permute-start.71 = (bf16[384,768]{1,0:T(8,128)(2,1)}, bf16[384,768]{1,0:T(8,128)(2,1)}, u32[]{:S(2)}, u32[]{:S(2)}) collective-permute-start(bf16[384,768]{1,0:T(8,128)(2,1)} %get-tuple-element.445), channel_id=1, source_target_pairs={{0,8},{4,12},{8,0},{12,4},{1,9},{5,13},{9,1},{13,5},{2,10},{6,14},... | collective-permute-start | bytes 1769480 | tf_op jit(solution)/shard_map/ppermute | solution.py:598
  472.9 27.0 %collective-permute-start.72 = (bf16[384,768]{1,0:T(8,128)(2,1)}, bf16[384,768]{1,0:T(8,128)(2,1)}, u32[]{:S(2)}, u32[]{:S(2)}) collective-permute-start(bf16[384,768]{1,0:T(8,128)(2,1)} %get-tuple-element.446), channel_id=1, source_target_pairs={{0,12},{4,8},{8,4},{12,0},{1,13},{5,9},{9,5},{13,1},{2,14},{6,10},... | collective-permute-start | bytes 1769480 | tf_op jit(solution)/shard_map/ppermute | solution.py:598
  (148 other events, 1420.3 us)
